TPU v7x, 256 devices: a whole 4x4x8 slice. The times are simulated.
256 devices in a mesh: seq: 32 (over y_hi, z, core), head: 8 (over y_lo, x).
Axes of the slice: x: 4, y: 4 (y_hi: 2, y_lo: 2; y = y_hi * 2 + y_lo), z: 8, core: 2. Of those that a mesh axis runs over, the one named last changes fastest.
Arguments:
- q_cells: bfloat16 [8192, 8192], P('seq', 'head'), may hold values from -60 to 60
- k_cells: bfloat16 [8192, 1024], P('seq', 'head'), may hold values from -11 to 11
- v_cells: bfloat16 [8192, 1024], P('seq', 'head'), may hold values from -6 to 6
- do_cells: bfloat16 [8192, 8192], P('seq', 'head'), may hold values from -6 to 6
- q_head: bfloat16 [1024, 8192], P('seq', 'head'), may hold values from -60 to 60
- k_head: bfloat16 [1024, 1024], P('seq', 'head'), may hold values from -6 to 6
- v_head: bfloat16 [1024, 1024], P('seq', 'head'), may hold values from -6 to 6
- do_head: bfloat16 [1024, 8192], P('seq', 'head'), may hold values from -6 to 6
- vis_mask: int32 [64, 8], P('seq'), may hold values from 0 to 1, as said below
Outputs:
- dq_cells: bfloat16 [8192, 8192], P('seq', 'head')
- dk_cells: bfloat16 [8192, 1024], P('seq', 'head')
- dv_cells: bfloat16 [8192, 1024], P('seq', 'head')
- dq_head: bfloat16 [1024, 8192], P('seq', 'head')
- dk_head: bfloat16 [1024, 1024], P('seq', 'head')
- dv_head: bfloat16 [1024, 1024], P('seq', 'head')
Inputs may be any that keep to these rules, and one draw needn't show every extreme that they name: vis_mask[b, t] = 1 lets the cells of block b see the headers of block t.
All inputs are finite; a program needn't handle non-finite values.
Results may differ from a plain program's by a relative error of at most 0.012.
Values may be sent and summed in bfloat16 or wider, within the bound.
A program may use at most 64 MiB of HBM per device.

v0:
```python
from functools import partial

import jax
import jax.numpy as jnp
from jax import lax
from jax.sharding import PartitionSpec as P

HD = 128
W = 256
BLOCK = 128


masked_score = -1e30


def product(pattern, former, latter):
    return jnp.einsum(pattern, former, latter, preferred_element_type=jnp.float32)


def block_stats(queries, key_rows, visible, scaling):
    scores = product("nkgd,mkd->kgnm", queries, key_rows) * scaling
    kept_scores = jnp.where(visible, scores, masked_score)
    highest = jnp.max(kept_scores, axis=-1)
    totals = jnp.sum(jnp.where(visible, jnp.exp(scores - highest[..., None]), 0.0), axis=-1)
    return (highest, totals)


def merge_stats(former, latter):
    highest = jnp.maximum(former[0], latter[0])
    return (
        highest,
        former[1] * jnp.exp(former[0] - highest) + latter[1] * jnp.exp(latter[0] - highest),
    )


def weights_of(queries, key_rows, log_totals, visible, scaling):
    scores = product("nkgd,mkd->kgnm", queries, key_rows) * scaling
    return jnp.where(visible, jnp.exp(scores - log_totals[..., None]), 0.0)


def block_delta(queries, grads_out, key_rows, value_rows, log_totals, visible, scaling):
    weights = weights_of(queries, key_rows, log_totals, visible, scaling)
    slopes = product("nkgd,mkd->kgnm", grads_out, value_rows)
    return jnp.sum(weights * slopes, axis=-1)


def block_grads(queries, grads_out, key_rows, value_rows, log_totals, deltas, visible, scaling):
    weights = weights_of(queries, key_rows, log_totals, visible, scaling)
    slopes = product("nkgd,mkd->kgnm", grads_out, value_rows)
    score_grads = weights * (slopes - deltas[..., None])
    weight_low = weights.astype(jnp.bfloat16)
    grad_low = score_grads.astype(jnp.bfloat16)
    grad_values = product("kgnm,nkgd->mkd", weight_low, grads_out)
    grad_keys = product("kgnm,nkgd->mkd", grad_low, queries) * scaling
    grad_queries = product("kgnm,mkd->nkgd", grad_low, key_rows) * scaling
    return (grad_queries, grad_keys, grad_values)


def to_rows(values):
    return jnp.transpose(values, (1, 2, 0, 3)).reshape(values.shape[1], values.shape[2], -1)


def from_rows(values, pieces):
    return jnp.transpose(values.reshape(values.shape[0], values.shape[1], pieces, -1), (2, 0, 1, 3))


def guarded(function, operands):
    return function(*operands)


def per_device(q_cells, k_cells, v_cells, do_cells, q_head, k_head, v_head, do_head, vis_mask):
    cell_count = q_cells.shape[0]
    kv_local = k_cells.shape[1] // HD
    query_local = q_cells.shape[1] // HD
    groups = query_local // kv_local
    scaling = HD ** (-0.5)
    regions = cell_count // W
    own_rows = q_head.shape[0]
    head_keys, head_values = (
        lax.all_gather(k_head, "seq", axis=0, tiled=True),
        lax.all_gather(v_head, "seq", axis=0, tiled=True),
    )
    all_queries, all_grads = (
        lax.all_gather(q_head, "seq", axis=0, tiled=True),
        lax.all_gather(do_head, "seq", axis=0, tiled=True),
    )
    header_count = head_keys.shape[0]
    blocks = header_count // BLOCK
    cell_query = q_cells.reshape(cell_count, kv_local, groups, HD)
    cell_grad = do_cells.reshape(cell_count, kv_local, groups, HD)
    cell_key = k_cells.reshape(cell_count, kv_local, HD)
    cell_value = v_cells.reshape(cell_count, kv_local, HD)
    region_query = q_cells.reshape(regions, W, kv_local, groups, HD)
    region_grad = do_cells.reshape(regions, W, kv_local, groups, HD)
    region_key = k_cells.reshape(regions, W, kv_local, HD)
    region_value = v_cells.reshape(regions, W, kv_local, HD)
    header_key_rows = head_keys.reshape(header_count, kv_local, HD)
    header_value_rows = head_values.reshape(header_count, kv_local, HD)
    key_blocks = head_keys.reshape(blocks, BLOCK, kv_local, HD)
    value_blocks = head_values.reshape(blocks, BLOCK, kv_local, HD)
    seen_blocks = jnp.transpose(jnp.repeat(vis_mask, BLOCK, axis=0) > 0)

    def outer_stat(operands):
        key_block, seen_column = operands
        return guarded(
            partial(block_stats, cell_query, scaling=scaling), (key_block, seen_column[:, None])
        )

    block_highest, block_totals = lax.map(outer_stat, (key_blocks, seen_blocks))
    outer_highest = jnp.max(block_highest, axis=0)
    outer_totals = jnp.sum(block_totals * jnp.exp(block_highest - outer_highest), axis=0)
    local_stats = jax.vmap(partial(block_stats, visible=True, scaling=scaling))(
        region_query, region_key
    )
    highest, totals = merge_stats(
        (to_rows(local_stats[0]), to_rows(local_stats[1])), (outer_highest, outer_totals)
    )
    cell_log = highest + jnp.log(totals)
    region_log = from_rows(cell_log, regions)

    def outer_delta(operands):
        key_block, value_block, seen_column = operands
        return guarded(
            partial(block_delta, cell_query, cell_grad, scaling=scaling),
            (key_block, value_block, cell_log, seen_column[:, None]),
        )

    local_delta = to_rows(
        jax.vmap(partial(block_delta, visible=True, scaling=scaling))(
            region_query, region_grad, region_key, region_value, region_log
        )
    )
    cell_delta = local_delta + jnp.sum(
        lax.map(outer_delta, (key_blocks, value_blocks, seen_blocks)), axis=0
    )
    query_zeros = jnp.zeros((cell_count, kv_local, groups, HD), jnp.float32)

    def outer_grad(running, operands):
        key_block, value_block, seen_column = operands
        gradients = guarded(
            partial(block_grads, cell_query, cell_grad, scaling=scaling),
            (key_block, value_block, cell_log, cell_delta, seen_column[:, None]),
        )
        return (running + gradients[0], (gradients[1], gradients[2]))

    outer_query, (key_parts, value_parts) = lax.scan(
        outer_grad, query_zeros, (key_blocks, value_blocks, seen_blocks)
    )
    local_grads = jax.vmap(partial(block_grads, visible=True, scaling=scaling))(
        region_query,
        region_grad,
        region_key,
        region_value,
        region_log,
        from_rows(cell_delta, regions),
    )
    query_blocks = all_queries.reshape(blocks, BLOCK, kv_local, groups, HD)
    grad_blocks = all_grads.reshape(blocks, BLOCK, kv_local, groups, HD)
    own_query = q_head.reshape(own_rows, kv_local, groups, HD)
    own_grad = do_head.reshape(own_rows, kv_local, groups, HD)
    first_row = lax.axis_index("seq") * own_rows

    def own_slice(values):
        return lax.dynamic_slice_in_dim(values, first_row, own_rows, 2)

    def own_update(values, replaced):
        return lax.dynamic_update_slice_in_dim(values, replaced, first_row, 2)

    cross_stats = lax.map(
        lambda operands: block_stats(operands, cell_key, True, scaling), query_blocks
    )
    cross_highest = to_rows(cross_stats[0])
    cross_totals = to_rows(cross_stats[1])
    self_stats = block_stats(own_query, header_key_rows, True, scaling)
    own_merged = merge_stats((own_slice(cross_highest), own_slice(cross_totals)), self_stats)
    part_highest = own_update(cross_highest, own_merged[0])
    part_totals = own_update(cross_totals, own_merged[1])
    head_highest = lax.pmax(part_highest.astype(jnp.bfloat16), "seq").astype(part_highest.dtype)
    head_totals = lax.psum(part_totals * jnp.exp(part_highest - head_highest), "seq")
    head_log = head_highest + jnp.log(head_totals)
    block_log = from_rows(head_log, blocks)
    own_log = own_slice(head_log)
    cross_delta = to_rows(
        lax.map(
            lambda operands: block_delta(
                operands[0], operands[1], cell_key, cell_value, operands[2], True, scaling
            ),
            (query_blocks, grad_blocks, block_log),
        )
    )
    self_delta = block_delta(
        own_query, own_grad, header_key_rows, header_value_rows, own_log, True, scaling
    )
    part_delta = own_update(cross_delta, own_slice(cross_delta) + self_delta)
    head_delta = lax.psum(part_delta, "seq")
    block_deltas = from_rows(head_delta, blocks)
    own_delta = own_slice(head_delta)
    key_zeros = jnp.zeros((cell_count, kv_local, HD), jnp.float32)

    def cross_grad(running, operands):
        gradients = block_grads(
            operands[0], operands[1], cell_key, cell_value, operands[2], operands[3], True, scaling
        )
        return ((running[0] + gradients[1], running[1] + gradients[2]), gradients[0])

    (cross_key, cross_value), cross_query = lax.scan(
        cross_grad, (key_zeros, key_zeros), (query_blocks, grad_blocks, block_log, block_deltas)
    )
    self_grads = block_grads(
        own_query, own_grad, header_key_rows, header_value_rows, own_log, own_delta, True, scaling
    )
    query_part = cross_query.reshape(header_count, query_local * HD)
    key_part = key_parts.reshape(header_count, kv_local * HD) + self_grads[1].reshape(
        header_count, kv_local * HD
    )
    value_part = value_parts.reshape(header_count, kv_local * HD) + self_grads[2].reshape(
        header_count, kv_local * HD
    )
    whole_sums = lax.psum((query_part, key_part, value_part), "seq")
    query_sum, key_sum, value_sum = [
        lax.dynamic_slice_in_dim(summed, first_row, own_rows, 0) for summed in whole_sums
    ]
    dq_cells = (
        local_grads[0].reshape(cell_count, query_local * HD)
        + outer_query.reshape(cell_count, query_local * HD)
    ).astype(jnp.bfloat16)
    dk_cells = (
        local_grads[1].reshape(cell_count, kv_local * HD)
        + cross_key.reshape(cell_count, kv_local * HD)
    ).astype(jnp.bfloat16)
    dv_cells = (
        local_grads[2].reshape(cell_count, kv_local * HD)
        + cross_value.reshape(cell_count, kv_local * HD)
    ).astype(jnp.bfloat16)
    dq_head = (query_sum + self_grads[0].reshape(own_rows, query_local * HD)).astype(jnp.bfloat16)
    return (
        dq_cells,
        dk_cells,
        dv_cells,
        dq_head,
        key_sum.astype(jnp.bfloat16),
        value_sum.astype(jnp.bfloat16),
    )


def solution(mesh):
    return jax.shard_map(
        per_device,
        mesh=mesh,
        in_specs=(
            P("seq", "head"),
            P("seq", "head"),
            P("seq", "head"),
            P("seq", "head"),
            P("seq", "head"),
            P("seq", "head"),
            P("seq", "head"),
            P("seq", "head"),
            P("seq", None),
        ),
        out_specs=(
            P("seq", "head"),
            P("seq", "head"),
            P("seq", "head"),
            P("seq", "head"),
            P("seq", "head"),
            P("seq", "head"),
        ),
        check_vma=False,
    )
```

profile of v0, /device:TPU:1, one launch (start us, length us, event | category | flops | bytes accessed | tf_op | source)
XLA Modules:
  0.0 988.0 jit_solution(11837171689813258582)
XLA Ops:
  9.5 47.2 %all_gather.12 = bf16[1024,128]{1,0:T(8,128)(2,1)S(1)} all-gather(bf16[32,128]{1,0:T(8,128)(2,1)} %param.26), channel_id=1, replica_groups=mesh['seq'=32,'head'=8] {'seq'}, dimensions={0}, use_global_device_ids=true | all-gather | bytes 270336 | tf_op jit(solution)/shard_map/all_gather | solution.py:80
  56.7 40.4 %all_gather.13 = bf16[1024,128]{1,0:T(8,128)(2,1)} all-gather(bf16[32,128]{1,0:T(8,128)(2,1)} %param.27), channel_id=1, replica_groups=mesh['seq'=32,'head'=8] {'seq'}, dimensions={0}, use_global_device_ids=true | all-gather | bytes 270336 | tf_op jit(solution)/shard_map/all_gather | solution.py:81
  98.7 4.6 while.74
  104.2 1.5 bitcast_reduce_fusion
  109.0 16.5 %while.75 = (s32[]{:T(128)}, f32[8,1,8,256]{3,2,1,0:T(8,128)}, pred[8,256]{1,0:T(8,128)(4,1)S(1)}, bf16[8,128,1,128]{3,1,2,0:T(8,128)(2,1)S(1)}, bf16[256,1,8,12...) while((s32[]{:T(128)}, f32[8,1,8,256]{3,2,1,0:T(8,128)}, ...), condition=%wide.region_11.12_spmd, body=%wide.region_9.11_spmd.sunk | while | flops 135526400 | bytes 3245173 | solution.py:134
  125.5 1.4 reduce_sum.103
  127.8 3.0 fusion.95
  133.0 2.2 copy.97
  135.3 1.9 copy.67
  137.2 37.2 %all-gather.5.cloned.1.call-done = bf16[1024,1024]{1,0:T(8,128)(2,1)} async-done(((bf16[32,1024]{1,0:T(8,128)(2,1)}), bf16[1024,1024]{1,0:T(8,128)(2,1)}) %all-gather.5.cloned.1.call-update) | async-done | bytes 2097168 | tf_op jit(solution)/shard_map/all_gather | solution.py:85
  174.4 2.2 copy.98
  176.6 1.9 copy.68
  179.8 18.8 %while.76 = (s32[]{:T(128)}, f32[8,1,8,128]{3,2,1,0:T(8,128)}, f32[8,1,8,128]{3,2,1,0:T(8,128)}, bf16[8,128,1,8,128]{4,1,3,2,0:T(8,128)(2,1)}, bf16[256,1,128]{2,0,1:T(8,128)(2,1)S(1)}, /*index=5*/s32[]{:T(128)}) while((s32[]{:T(128)}, f32[8,1,8,128]{3,2,1,0:T(8,128)}, f32[8,1,8,128]{3,2,1,0:T(8,128)}, ...), condition=%wide.region_18.19_spmd, body=%wide.region_15.18_spmd.sunk | while | flops 68155392 | bytes 2453589 | solution.py:169
  179.8 1.4 fusion.227
  182.1 1.3 fusion.227
  184.5 1.3 fusion.227
  186.8 1.4 fusion.227
  189.1 1.3 fusion.227
  191.5 1.3 fusion.227
  193.8 1.3 fusion.227
  196.2 1.4 fusion.227
  198.5 1.4 fusion.157
  199.9 1.5 dynamic_update_slice.41
  201.4 1.5 dynamic_update_slice.40
  202.8 1.4 convert_element_type.50
  204.2 124.3 %pmax.7 = bf16[1,8,1024]{2,1,0:T(8,128)(2,1)} all-reduce(bf16[1,8,1024]{2,1,0:T(8,128)(2,1)} %convert_element_type.50), channel_id=1, replica_groups=mesh['seq'=32,'head'=8] {'seq'}, use_global_device_ids=true, to_apply=%region_20.21 | all-reduce | flops 8192 | bytes 32768 | tf_op jit(solution)/shard_map/pmax | solution.py:178
  328.5 1.4 fusion.148
  329.9 128.5 %psum.35 = f32[1,8,1024]{2,1,0:T(8,128)} all-reduce(f32[1,8,1024]{2,1,0:T(8,128)} %fusion.148), channel_id=1, replica_groups=mesh['seq'=32,'head'=8] {'seq'}, use_global_device_ids=true, to_apply=%region_22.23 | all-reduce | flops 8192 | bytes 65536 | tf_op jit(solution)/shard_map/psum | solution.py:179
  460.5 31.5 %while.77 = (s32[]{:T(128)}, f32[8,1,8,128]{3,2,1,0:T(8,128)}, bf16[8,128,1,8,128]{4,1,3,2,0:T(8,128)(2,1)}, bf16[256,1,128]{2,0,1:T(8,128)(2,1)S(1)}, f32[8,1,8...) while((s32[]{:T(128)}, f32[8,1,8,128]{3,2,1,0:T(8,128)}, ...), condition=%wide.region_25.26_spmd, body=%wide.region_23.25_spmd.sunk | while | flops 135265280 | bytes 2777197 | solution.py:184
  462.4 1.4 fusion.233
  466.4 1.4 fusion.233
  470.3 1.4 fusion.233
  474.2 1.4 fusion.233
  478.2 1.4 fusion.233
  482.1 1.4 fusion.233
  486.0 1.4 fusion.233
  490.0 1.4 fusion.233
  491.9 2.6 multiply_reduce_fusion
  494.5 1.4 bitcast_add_fusion.1
  495.9 1.5 dynamic_update_slice.42
  497.3 128.5 %psum.36 = f32[1,8,1024]{2,1,0:T(8,128)} all-reduce(f32[1,8,1024]{2,1,0:T(8,128)} %dynamic_update_slice.42), channel_id=1, replica_groups=mesh['seq'=32,'head'=8] {'seq'}, use_global_device_ids=true, to_apply=%region_27.28 | all-reduce | flops 8192 | bytes 65536 | tf_op jit(solution)/shard_map/psum | solution.py:195
  625.9 63.3 %while.79 = (s32[]{:T(128)}, f32[256,1,128]{0,2,1:T(8,128)}, f32[256,1,128]{0,2,1:T(8,128)}, f32[8,128,1,8,128]{4,3,1,0,2:T(8,128)}, bf16[8,128,1,8,128]{4,1,3,2...) while((s32[]{:T(128)}, f32[256,1,128]{0,2,1:T(8,128)}, ...), condition=%wide.region_29.30_spmd.clone, body=%wide.region_28.29_spmd.clone.sunk | while | flops 337412096 | bytes 9134296 | solution.py:206
  627.9 1.9 fusion.262
  635.8 1.9 fusion.262
  642.4 1.3 fusion.259
  643.7 1.9 fusion.262
  650.3 1.3 fusion.259
  651.6 1.9 fusion.262
  658.2 1.3 fusion.259
  659.5 1.9 fusion.262
  667.4 1.9 fusion.262
  675.4 1.9 fusion.262
  683.3 1.9 fusion.262
  689.2 5.1 copy.144
  694.9 39.1 %while.78 = (s32[]{:T(128)}, f32[256,1,8,128]{0,3,2,1:T(8,128)}, f32[8,128,1,128]{3,1,2,0:T(8,128)}, f32[8,128,1,128]{3,1,2,0:T(8,128)}, bf16[8,128,1,128]{3,1,2...) while((s32[]{:T(128)}, f32[256,1,8,128]{0,3,2,1:T(8,128)}, ...), condition=%wide.region_14.15_spmd.clone, body=%wide.region_13.14_spmd.clone.sunk | while | flops 338182144 | bytes 17548512 | solution.py:146
  734.1 2.5 copy.83
  736.6 2.1 fusion.114
  738.7 1.4 convolution_multiply_fusion.8
  740.1 2.5 copy.60
  742.7 2.6 add_convert_fusion
  749.5 140.0 %all-reduce.5 = (bf16[1024,128]{1,0:T(8,128)(2,1)S(1)}, bf16[1024,128]{1,0:T(8,128)(2,1)}) all-reduce(f32[1024,128]{1,0:T(8,128)} %fusion.104, f32[1024,128]{1,0:T(8,128)} %fusion.105), channel_id=1, replica_groups=mesh['seq'=32,'head'=8] {'seq'}, use_global_device_ids=true, to_apply=%region_31.32 | all-reduce | flops 262144 | bytes 1572864 | tf_op jit(solution)/shard_map/psum | solution.py:219
  890.8 2.4 fusion.111
  894.4 85.6 %all-reduce.4.cloned.1.call-done = f32[1024,1024]{1,0:T(8,128)} async-done(((f32[1024,1024]{1,0:T(8,128)}), f32[1024,1024]{1,0:T(8,128)}) %all-reduce.4.cloned.1.call-update) | async-done | bytes 4194320 | tf_op jit(solution)/shard_map/psum | solution.py:219
  979.9 1.6 fusion.135
  (362 shorter events, 153.0 us)
Async XLA Ops:
  7.2 125.9 %all-gather.3.cloned.1.call-start = ((), (), s32[]{:S(2)}) async-start(), calls=%async_computation | async-start | bytes 2162688 | tf_op jit(solution)/shard_map/all_gather | solution.py:84
  7.9 166.5 %all-gather.5.cloned.1.call-start = ((), (), s32[]{:S(2)}) async-start(), calls=%async_computation.1 | async-start | bytes 2162688 | tf_op jit(solution)/shard_map/all_gather | solution.py:85
  8.6 971.3 %all-reduce.4.cloned.1.call-start = ((), (), s32[]{:S(2)}) async-start(), calls=%async_computation.2 | async-start | bytes 8388608 | tf_op jit(solution)/shard_map/psum | solution.py:219
  98.7 4.6 copy-start.9
  103.3 0.6 copy-start.15
  103.3 0.9 copy-start.2
  105.7 1.5 copy-start.23
  106.4 1.3 copy-start.24
  107.2 1.8 copy-start.26
  107.6 1.4 copy-start.25
  109.0 18.7 %copy-start.5 = (bf16[256,128]{1,0:T(8,128)(2,1)S(1)}, bf16[256,128]{1,0:T(8,128)(2,1)}, u32[]{:S(2)}) copy-start(bf16[256,128]{1,0:T(8,128)(2,1)} %param.23) | copy-start | bytes 196612
  125.5 5.2 copy-start.19
  127.8 3.0 copy-start.21
  127.8 3.0 copy-start.29
  127.8 3.0 copy-start.16
  131.2 1.0 copy-start.3
  131.2 1.0 copy-start.27
  459.2 1.3 copy-start.18
  626.6 4.5 copy-start.6
  632.3 1.4 copy-start.7
  634.5 4.5 copy-start.6
  640.2 1.4 copy-start.7
  642.4 4.5 copy-start.6
  648.2 1.4 copy-start.7
  650.3 4.5 copy-start.6
  656.1 1.4 copy-start.7
  658.2 4.5 copy-start.6
  664.0 1.4 copy-start.7
  666.1 4.5 copy-start.6
  671.9 1.4 copy-start.7
  674.1 4.5 copy-start.6
  679.8 1.4 copy-start.7
  682.0 4.5 copy-start.6
  687.7 1.4 copy-start.7
  694.3 0.7 copy-start.20
  695.3 3.0 copy-start
  698.8 1.1 copy-start.1
  700.2 3.0 copy-start
  703.7 1.1 copy-start.1
  705.1 3.0 copy-start
  708.6 1.1 copy-start.1
  710.0 3.0 copy-start
  713.5 1.1 copy-start.1
  714.9 3.0 copy-start
  718.3 1.1 copy-start.1
  719.8 3.0 copy-start
  723.2 1.1 copy-start.1
  724.7 3.0 copy-start
  728.1 1.1 copy-start.1
  729.6 3.0 copy-start
  733.0 1.1 copy-start.1
  734.1 2.5 copy-start.22
  738.7 1.4 copy-start.12
  740.1 6.0 copy-start.28
  742.7 3.5 copy-start.4
  742.7 3.5 copy-start.13
  745.3 1.5 copy-start.17
  745.3 1.5 copy-start.31
  746.4 1.6 copy-start.14
  746.5 1.6 copy-start.30
  746.9 2.4 copy-start.8
  746.9 2.5 copy-start.11
  749.3 143.9 %copy-start.10 = (bf16[256,1024]{1,0:T(8,128)(2,1)S(1)}, bf16[256,1024]{1,0:T(8,128)(2,1)}, u32[]{:S(2)}) copy-start(bf16[256,1024]{1,0:T(8,128)(2,1)} %param.24) | copy-start | bytes 1572868
Sparse Core Ops, SparseCore 0:
  10.8 84.3 all-gather.2
  98.0 76.3 all-gather.4
  694.4 285.4 all-reduce.3
where the time goes:
time: 992 us; the launch traced here: 988 us
  blocking collectives  609 us (61%)
  matrix products  139 us (14%)
  waiting for transfers between devices  124 us (12%)
  local copies, waits for them, and re-layouts  76.3 us (8%)
  other arithmetic  23.8 us (2%)
  between operations  14.2 us (1%)
    psum x1, blocking collectives, per_device(): whole_sums = lax.psum((query_part, key_part, value_part), 'seq')  140 us
    dot_general x138, matrix products, product(): jnp.einsum(pattern, former, latter, preferred_element_type=jnp.float32)  139 us
    psum x1, blocking collectives, per_device(): head_delta = lax.psum(part_delta, 'seq')  129 us
    psum x1, blocking collectives, per_device(): lax.psum(part_totals * jnp.exp(part_highest - head_highest), 'seq')  128 us
    pmax x1, blocking collectives, per_device(): lax.pmax(part_highest.astype(jnp.bfloat16), 'seq')  124 us
    psum x1, waiting for transfers between devices, per_device(): whole_sums = lax.psum((query_part, key_part, value_part), 'seq')  85.6 us
    all_gather x1, blocking collectives, per_device(): lax.all_gather(k_head, 'seq', axis=0, tiled=True)  47.2 us
    all_gather x1, blocking collectives, per_device(): lax.all_gather(v_head, 'seq', axis=0, tiled=True)  40.4 us
  transfers between devices with their start and end apart: 3, of which 2 were waited for; matrix products, arithmetic and copies ran while one was open for 9% of the time, Pallas kernels for 0%

commit v1 on v0

v1 whole, which is shorter than its diff:
```python
from functools import partial

import jax
import jax.numpy as jnp
from jax import lax
from jax.experimental import pallas as pl
from jax.experimental.pallas import tpu as pltpu
from jax.sharding import PartitionSpec as P

HD = 128
BLOCK = 128
LOG2E = 1.4426950408889634
HIDDEN = -1e30
MESH = pl.DeviceIdType.MESH
F32 = jnp.float32
BF16 = jnp.bfloat16


def dot_nt(a, b):
    return lax.dot_general(a, b, (((1,), (1,)), ((), ())), preferred_element_type=F32)


def dot_nn(a, b):
    return jnp.dot(a, b, preferred_element_type=F32)


def fold_max(x):
    return jnp.max(x.reshape(x.shape[0] // 8, 8, x.shape[1]), axis=0)


def fold_sum(x):
    return jnp.sum(x.reshape(x.shape[0] // 8, 8, x.shape[1]), axis=0)


def turned(x):
    return jnp.transpose(x.astype(F32)).astype(BF16)


def kernel(
    ring,
    mask_ref, qc, kc, vc, doc, qh, kh, vh, doh,
    dqc_o, dkc_o, dvc_o, dqh_o, dkh_o, dvh_o,
    kvc, kvh, qdo, ktc, kth, kts, bias_s, e_c, dp_c, e_h, dp_h, st, st_f, st_d,
    acc_h, acc_c, dqp, dq_own, dq_r, xh_r, xc_r, yh_s, yh_r, yc_s, yc_r, zh_s, zh_r,
    a_s, a_r, q_s, q_r, t_s, t_r, d_s, d_r, z_s, z_r, i_s, i_r,
):
    cells = qc.shape[0]
    rows = qh.shape[0]
    heads = qc.shape[1] // HD
    wide = heads * HD
    scale = HD ** (-0.5)
    factor = scale * LOG2E
    me = lax.axis_index("seq")
    hx = lax.axis_index("head")
    core = me % 2
    pos_z = (me // 2) % ring
    pos_y = me // (2 * ring)

    def peer(a, d, b):
        y = (pos_y + a) % 2
        z = (pos_z + d + ring) % ring
        c = (core + b) % 2
        return ((y * ring + z) * 2 + c, hx)

    def rcopy(src, dst, send, recv, to):
        return pltpu.make_async_remote_copy(
            src_ref=src, dst_ref=dst, send_sem=send, recv_sem=recv,
            device_id=to, device_id_type=MESH,
        )

    barrier = pltpu.get_barrier_semaphore()
    for d in range(1, ring):
        pl.semaphore_signal(barrier, inc=1, device_id=peer(0, d, 0), device_id_type=MESH)
    pl.semaphore_signal(barrier, inc=1, device_id=peer(1, 0, 0), device_id_type=MESH)
    pl.semaphore_signal(barrier, inc=1, device_id=peer(0, 0, 1), device_id_type=MESH)

    kvh[0, 0:rows, 0:HD] = kh[...]
    kvh[0, 0:rows, HD : 2 * HD] = vh[...]
    kvc[0, :, 0:HD] = kc[...]
    kvc[0, :, HD : 2 * HD] = vc[...]
    qdo[0:rows, 0:wide] = qh[...]
    qdo[0:rows, wide : 2 * wide] = doh[...]

    pl.semaphore_wait(barrier, ring + 1)

    order = []
    for d in range(1, ring // 2 + 1):
        order.append(d)
        if ring - d != d:
            order.append(ring - d)

    a_cp = {}
    for d in order:
        a_cp[d] = rcopy(
            kvh.at[0, pl.ds(0, rows)], kvh.at[0, pl.ds(d * rows, rows)],
            a_s.at[d], a_r.at[d], peer(0, d, 0),
        )
        a_cp[d].start()
    c_y = rcopy(kvc.at[0], kvc.at[2], i_s.at[0], i_r.at[0], peer(1, 0, 0))
    c_y.start()
    c_c = rcopy(kvc.at[0], kvc.at[1], i_s.at[1], i_r.at[1], peer(0, 0, 1))
    c_c.start()
    q_cp = {}
    for d in order:
        q_cp[d] = rcopy(
            qdo.at[pl.ds(0, rows)], qdo.at[pl.ds(d * rows, rows)],
            q_s.at[d], q_r.at[d], peer(0, d, 0),
        )
        q_cp[d].start()

    lane = lax.broadcasted_iota(jnp.int32, (1, cells), 1)
    for a in range(2):
        for d in range(ring):
            y = (pos_y + a) % 2
            z = (pos_z - d + ring) % ring
            block = (y * ring + z) * 2 * rows // BLOCK
            low = jnp.where(mask_ref[0, block] > 0, 0.0, HIDDEN)
            high = jnp.where(mask_ref[1, block] > 0, 0.0, HIDDEN)
            bias_s[a * ring + d : a * ring + d + 1, :] = jnp.where(lane < BLOCK, low, high)
    acc_h[...] = jnp.zeros_like(acc_h)
    acc_c[...] = jnp.zeros_like(acc_c)
    ktc[0] = turned(kvc[0, :, 0:HD])

    for d in order:
        a_cp[d].wait_recv()
    h_y = rcopy(kvh.at[0], kvh.at[2], i_s.at[3], i_r.at[3], peer(1, 0, 0))
    h_y.start()
    h_c = rcopy(kvh.at[0], kvh.at[1], i_s.at[4], i_r.at[4], peer(0, 0, 1))
    h_c.start()
    c_y.wait_recv()
    c_f = rcopy(kvc.at[2], kvc.at[3], i_s.at[2], i_r.at[2], peer(0, 0, 1))
    c_f.start()
    kth[0] = turned(kvh[0, :, 0:HD])
    h_y.wait_recv()
    h_f = rcopy(kvh.at[2], kvh.at[3], i_s.at[5], i_r.at[5], peer(0, 0, 1))
    h_f.start()
    h_c.wait_recv()
    kth[1] = turned(kvh[1, :, 0:HD])
    kth[2] = turned(kvh[2, :, 0:HD])
    h_f.wait_recv()
    kth[3] = turned(kvh[3, :, 0:HD])

    half = ring * rows // 2
    per = half // rows

    def cell_head(h, carry):
        col = pl.ds(pl.multiple_of(h * HD, HD), HD)
        q = qc[:, col]
        g = doc[:, col]
        top = fold_max(dot_nt(kvc[0, :, 0:HD], q))
        for ab in range(4):
            for p in range(2):
                s = dot_nt(kvh[ab, p * half : (p + 1) * half, 0:HD], q)
                for j in range(per):
                    at = (ab // 2) * ring + p * per + j
                    top = jnp.maximum(
                        top, fold_max(s[j * rows : (j + 1) * rows]) + bias_s[at : at + 1, :]
                    )
        m2 = jnp.max(top, axis=0, keepdims=True) * factor
        s = dot_nt(kvc[0, :, 0:HD], q)
        dp = dot_nt(kvc[0, :, HD : 2 * HD], g)
        e = jnp.exp2(s * factor - m2)
        total = fold_sum(e)
        inner = fold_sum(e * dp)
        e_c[0:cells, :] = e
        dp_c[0:cells, :] = dp
        for ab in range(4):
            for p in range(2):
                s = dot_nt(kvh[ab, p * half : (p + 1) * half, 0:HD], q)
                dp = dot_nt(kvh[ab, p * half : (p + 1) * half, HD : 2 * HD], g)
                base = cells + (2 * ab + p) * half
                dp_c[base : base + half, :] = dp
                for j in range(per):
                    at = (ab // 2) * ring + p * per + j
                    part = slice(j * rows, (j + 1) * rows)
                    e = jnp.exp2(s[part] * factor - (m2 - bias_s[at : at + 1, :]))
                    total = total + fold_sum(e)
                    inner = inner + fold_sum(e * dp[part])
                    e_c[base + j * rows : base + (j + 1) * rows, :] = e
        inv = 1.0 / jnp.sum(total, axis=0, keepdims=True)
        delta = jnp.sum(inner, axis=0, keepdims=True) * inv
        w = e_c[0:cells, :] * inv
        ds = (w * (dp_c[0:cells, :] - delta)).astype(BF16)
        acc_c[0, 0:cells, 0:HD] += dot_nn(ds, q)
        acc_c[0, 0:cells, HD : 2 * HD] += dot_nn(w.astype(BF16), g)
        dq = dot_nn(ktc[0], ds)
        size = 2 * half
        for ab in range(4):
            base = cells + ab * size
            w = e_c[base : base + size, :] * inv
            ds = (w * (dp_c[base : base + size, :] - delta)).astype(BF16)
            acc_h[ab, :, 0:HD] += dot_nn(ds, q)
            acc_h[ab, :, HD : 2 * HD] += dot_nn(w.astype(BF16), g)
            dq = dq + dot_nn(kth[ab], ds)
        dqc_o[:, col] = (jnp.transpose(dq) * scale).astype(BF16)
        return carry

    lax.fori_loop(0, heads, cell_head, 0)

    hx_cp = []
    for a in range(2):
        cp = rcopy(acc_h.at[2 * a + 1], xh_r.at[a], i_s.at[6 + a], i_r.at[6 + a], peer(0, 0, 1))
        cp.start()
        hx_cp.append(cp)

    c_c.wait_recv()
    c_f.wait_recv()
    for ab in range(1, 4):
        ktc[ab] = turned(kvc[ab, :, 0:HD])
    for ab in range(4):
        kts[:, ab * rows : (ab + 1) * rows] = kth[ab, :, 0:rows]
    for d in order:
        q_cp[d].wait_recv()

    lines = ring * rows

    def head_stats(h, carry):
        col = pl.ds(pl.multiple_of(h * HD, HD), HD)
        col_g = pl.ds(pl.multiple_of(wide + h * HD, HD), HD)
        q = qdo[:, col]
        g = qdo[:, col_g]
        top = fold_max(dot_nt(kvc[0, :, 0:HD], q))
        for ab in range(1, 4):
            top = jnp.maximum(top, fold_max(dot_nt(kvc[ab, :, 0:HD], q)))
        for ab in range(4):
            top = jnp.maximum(top, fold_max(dot_nt(kvh[ab, 0:rows, 0:HD], q)))
        m2 = jnp.max(top, axis=0, keepdims=True) * factor
        total = jnp.zeros((8, lines), F32)
        inner = jnp.zeros((8, lines), F32)
        for ab in range(4):
            dp = dot_nt(kvc[ab, :, HD : 2 * HD], g)
            e = jnp.exp2(dot_nt(kvc[ab, :, 0:HD], q) * factor - m2)
            total = total + fold_sum(e)
            inner = inner + fold_sum(e * dp)
            e_h[h, ab * cells : (ab + 1) * cells, :] = e
            dp_h[h, ab * cells : (ab + 1) * cells, :] = dp
        for ab in range(4):
            base = 4 * cells + ab * rows
            dp = dot_nt(kvh[ab, 0:rows, HD : 2 * HD], g)
            e = jnp.exp2(dot_nt(kvh[ab, 0:rows, 0:HD], q) * factor - m2)
            total = total + fold_sum(e)
            inner = inner + fold_sum(e * dp)
            e_h[h, base : base + rows, :] = e
            dp_h[h, base : base + rows, :] = dp
        st[0, 0, pl.ds(h, 1), :] = m2
        st[0, 1, pl.ds(h, 1), :] = jnp.sum(total, axis=0, keepdims=True)
        st[0, 2, pl.ds(h, 1), :] = jnp.sum(inner, axis=0, keepdims=True)
        return carry

    lax.fori_loop(0, heads, head_stats, 0)

    t_cp = {}
    for d in order:
        t_cp[d] = rcopy(st.at[0], st.at[d], t_s.at[d], t_r.at[d], peer(0, d, 0))
        t_cp[d].start()

    for cp in hx_cp:
        cp.wait_recv()
    yh_s[...] = (acc_h[2] + xh_r[1]).astype(BF16)
    hy_cp = rcopy(yh_s, yh_r, i_s.at[8], i_r.at[8], peer(1, 0, 0))
    hy_cp.start()

    for d in order:
        t_cp[d].wait_recv()
    seen = [[st[0, k] for k in range(3)]]
    for d in range(1, ring):
        seen.append([pltpu.roll(st[d, k], d * rows, 1) for k in range(3)])
    best = seen[0][0]
    for d in range(1, ring):
        best = jnp.maximum(best, seen[d][0])
    total = jnp.zeros_like(best)
    inner = jnp.zeros_like(best)
    for d in range(ring):
        lift = jnp.exp2(seen[d][0] - best)
        total = total + seen[d][1] * lift
        inner = inner + seen[d][2] * lift
    inv = 1.0 / total
    st_f[...] = jnp.exp2(st[0, 0] - best) * inv
    st_d[...] = inner * inv

    hy_cp.wait_recv()
    own_h = acc_h[0] + xh_r[0] + yh_r[...].astype(F32)
    acc_h[0] = own_h
    zh_s[...] = own_h.astype(BF16)
    z_cp = {}
    for d in order:
        z_cp[d] = rcopy(
            zh_s.at[pl.ds(d * rows, rows)], zh_r.at[d], z_s.at[d], z_r.at[d], peer(0, -d, 0)
        )
        z_cp[d].start()

    def head_grads(h, carry):
        col = pl.ds(pl.multiple_of(h * HD, HD), HD)
        col_g = pl.ds(pl.multiple_of(wide + h * HD, HD), HD)
        q = qdo[:, col]
        g = qdo[:, col_g]
        f = st_f[pl.ds(h, 1), :]
        delta = st_d[pl.ds(h, 1), :]
        dq = jnp.zeros((HD, lines), F32)
        for ab in range(4):
            part = slice(ab * cells, (ab + 1) * cells)
            w = e_h[h, part, :] * f
            ds = (w * (dp_h[h, part, :] - delta)).astype(BF16)
            acc_c[ab, 0:cells, 0:HD] += dot_nn(ds, q)
            acc_c[ab, 0:cells, HD : 2 * HD] += dot_nn(w.astype(BF16), g)
            dq = dq + dot_nn(ktc[ab], ds)
        part = slice(4 * cells, 4 * cells + 4 * rows)
        w = e_h[h, part, :] * f
        ds = (w * (dp_h[h, part, :] - delta)).astype(BF16)
        dk = dot_nn(ds, q)
        dv = dot_nn(w.astype(BF16), g)
        for ab in range(4):
            acc_c[ab, cells : cells + rows, 0:HD] += dk[ab * rows : (ab + 1) * rows]
            acc_c[ab, cells : cells + rows, HD : 2 * HD] += dv[ab * rows : (ab + 1) * rows]
        dq = dq + dot_nn(kts[...], ds)
        flat = jnp.transpose(dq) * scale
        dq_own[:, col] = flat[0:rows]
        dqp[:, col] = flat.astype(BF16)
        for d in order:
            rcopy(
                dqp.at[pl.ds(d * rows, rows), col], dq_r.at[d, :, col],
                d_s.at[d], d_r.at[d], peer(0, -d, 0),
            ).start()
        return carry

    lax.fori_loop(0, heads, head_grads, 0)

    cx_cp = []
    for a in (1, 0):
        cp = rcopy(acc_c.at[2 * a + 1], xc_r.at[a], i_s.at[9 + a], i_r.at[9 + a], peer(0, 0, 1))
        cp.start()
        cx_cp.append(cp)
    cx_cp[0].wait_recv()
    yc_s[...] = (acc_c[2] + xc_r[1]).astype(BF16)
    cy_cp = rcopy(yc_s, yc_r, i_s.at[11], i_r.at[11], peer(1, 0, 0))
    cy_cp.start()

    for d in order:
        z_cp[d].wait_recv()
    own_h = acc_h[0, 0:rows]
    for d in range(1, ring):
        own_h = own_h + zh_r[d].astype(F32)
    cx_cp[1].wait_recv()
    own_c = acc_c[0] + xc_r[0]

    d_cp = {}
    for d in order:
        d_cp[d] = rcopy(
            dqp.at[pl.ds(d * rows, rows)], dq_r.at[d], d_s.at[d], d_r.at[d], peer(0, -d, 0)
        )
        d_cp[d].wait_recv()
    dq = dq_own[...]
    for d in range(1, ring):
        dq = dq + dq_r[d].astype(F32)
    dqh_o[...] = dq.astype(BF16)

    cy_cp.wait_recv()
    own_c = own_c + yc_r[...].astype(F32)
    dkc_o[...] = (own_c[0:cells, 0:HD] * scale).astype(BF16)
    dvc_o[...] = own_c[0:cells, HD : 2 * HD].astype(BF16)
    own_h = own_h + own_c[cells : cells + rows]
    dkh_o[...] = (own_h[:, 0:HD] * scale).astype(BF16)
    dvh_o[...] = own_h[:, HD : 2 * HD].astype(BF16)

    for group in (a_cp, q_cp, t_cp, z_cp, d_cp):
        for d in order:
            group[d].wait_send()
    for cp in [c_y, c_c, c_f, h_y, h_c, h_f, hy_cp, cy_cp] + hx_cp + cx_cp:
        cp.wait_send()


def per_device(ring, q_cells, k_cells, v_cells, do_cells, q_head, k_head, v_head, do_head, vis_mask):
    cells = q_cells.shape[0]
    rows = q_head.shape[0]
    wide = q_cells.shape[1]
    heads = wide // HD
    lines = ring * rows
    keys_c = cells + 4 * lines
    keys_h = 4 * cells + 4 * rows
    ext = cells + rows
    vmem = pl.BlockSpec(memory_space=pltpu.VMEM)
    dma = pltpu.SemaphoreType.DMA
    return pl.pallas_call(
        partial(kernel, ring),
        out_shape=[
            jax.ShapeDtypeStruct((cells, wide), BF16),
            jax.ShapeDtypeStruct((cells, HD), BF16),
            jax.ShapeDtypeStruct((cells, HD), BF16),
            jax.ShapeDtypeStruct((rows, wide), BF16),
            jax.ShapeDtypeStruct((rows, HD), BF16),
            jax.ShapeDtypeStruct((rows, HD), BF16),
        ],
        in_specs=[pl.BlockSpec(memory_space=pltpu.SMEM)] + [vmem] * 8,
        out_specs=[vmem] * 6,
        scratch_shapes=[
            pltpu.VMEM((4, cells, 2 * HD), BF16),
            pltpu.VMEM((4, lines, 2 * HD), BF16),
            pltpu.VMEM((lines, 2 * wide), BF16),
            pltpu.VMEM((4, HD, cells), BF16),
            pltpu.VMEM((4, HD, lines), BF16),
            pltpu.VMEM((HD, 4 * rows), BF16),
            pltpu.VMEM((2 * ring, cells), F32),
            pltpu.VMEM((keys_c, cells), F32),
            pltpu.VMEM((keys_c, cells), F32),
            pltpu.VMEM((heads, keys_h, lines), F32),
            pltpu.VMEM((heads, keys_h, lines), F32),
            pltpu.VMEM((ring, 3, heads, lines), F32),
            pltpu.VMEM((heads, lines), F32),
            pltpu.VMEM((heads, lines), F32),
            pltpu.VMEM((4, lines, 2 * HD), F32),
            pltpu.VMEM((4, ext, 2 * HD), F32),
            pltpu.VMEM((lines, wide), BF16),
            pltpu.VMEM((rows, wide), F32),
            pltpu.VMEM((ring, rows, wide), BF16),
            pltpu.VMEM((2, lines, 2 * HD), F32),
            pltpu.VMEM((2, ext, 2 * HD), F32),
            pltpu.VMEM((lines, 2 * HD), BF16),
            pltpu.VMEM((lines, 2 * HD), BF16),
            pltpu.VMEM((ext, 2 * HD), BF16),
            pltpu.VMEM((ext, 2 * HD), BF16),
            pltpu.VMEM((lines, 2 * HD), BF16),
            pltpu.VMEM((ring, rows, 2 * HD), BF16),
        ]
        + [dma((ring,))] * 10
        + [dma((12,))] * 2,
        compiler_params=pltpu.CompilerParams(
            collective_id=0, has_side_effects=True, vmem_limit_bytes=60 * 1024 * 1024
        ),
    )(vis_mask, q_cells, k_cells, v_cells, do_cells, q_head, k_head, v_head, do_head)


def solution(mesh):
    both = P("seq", "head")
    return jax.shard_map(
        partial(per_device, mesh.shape["seq"] // 4),
        mesh=mesh,
        in_specs=(both,) * 8 + (P("seq", None),),
        out_specs=(both,) * 6,
        check_vma=False,
    )
```

time: 992 us -> 74.5 us (0.08)
  blocking collectives: 609 us -> 0 us
  matrix products: 139 us -> 0 us
  waiting for transfers between devices: 124 us -> 0 us
  local copies, waits for them, and re-layouts: 76.3 us -> 5.62 us
  Pallas kernels: 0 us -> 67.5 us
  other arithmetic: 23.8 us -> 0 us
  between operations: 14.2 us -> 0.66 us
    psum x3 -> x0, blocking collectives: 397 us -> none  [the longest x1 140 us: per_device(): whole_sums = lax.psum((query_part, key_part, value_part), 'seq')]
    dot_general x138 -> x0, matrix products: 139 us -> none  [product(): jnp.einsum(pattern, former, latter, preferred_element_type=jnp.float32)]
    pmax x1 -> x0, blocking collectives: 124 us -> none  [per_device(): lax.pmax(part_highest.astype(jnp.bfloat16), 'seq')]
    all_gather x2 -> x0, blocking collectives: 87.6 us -> none  [the longest x1 47.2 us: per_device(): lax.all_gather(k_head, 'seq', axis=0, tiled=True)]
    psum x1 -> x0, waiting for transfers between devices: 85.6 us -> none  [per_device(): whole_sums = lax.psum((query_part, key_part, value_part), 'seq')]
    pallas_call x0 -> x1, Pallas kernels: none -> 67.5 us  [per_device(): pl.pallas_call(partial(kernel, ring), out_shape=[jax.ShapeDtypeStruct((ce...]
    all_gather x2 -> x0, waiting for transfers between devices: 37.2 us -> none  [the longest x1 37.2 us: per_device(): lax.all_gather(do_head, 'seq', axis=0, tiled=True)]
    dynamic_update_slice x43 -> x0, local copies, waits for them, and re-layouts: 27.9 us -> none  [the longest x16 9.64 us: per_device(): lax.map(lambda operands: block_stats(operands, cell_key, True, scaling),...]
  transfers between devices with their start and end apart: 3 -> 0, of which waited for: 2 -> 0; matrix products, arithmetic and copies ran while one was open for 9% -> 0% of each run, Pallas kernels for 0% -> 0%
where the time goes in v1:
time: 74.5 us; the launch traced here: 73.8 us
  Pallas kernels  67.5 us (91%)
  local copies, waits for them, and re-layouts  5.62 us (8%)
    pallas_call x1, Pallas kernels, per_device(): pl.pallas_call(partial(kernel, ring), out_shape=[jax.ShapeDtypeStruct((ce...  67.5 us
    unnamed x16, local copies, waits for them, and re-layouts  5.62 us

profile of v1, /device:TPU:1, one launch (start us, length us, event | category | flops | bytes accessed | tf_op | source)
XLA Modules:
  0.0 73.8 jit_solution(16539093163830658159)
XLA Ops:
  0.6 67.5 %shard_map.136 = (bf16[256,1024]{1,0:T(8,128)(2,1)}, bf16[256,128]{1,0:T(8,128)(2,1)}, bf16[256,128]{1,0:T(8,128)(2,1)}, bf16[32,1024]{1,0:T(8,128)(2,1)}, bf16[...) custom-call(s32[2,8]{1,0:T(2,128)} %mask_ref.1, bf16[256,1024]{1,0:T(8,128)(2,1)} %qc.1, bf16[256,128]{1,0:T(8,128)(2,1)} %kc.1, ...), custom_call_target="tpu_custom_call" | custom-call | tf_op jit(solution)/shard_map/pallas_call | solution.py:383
  68.2 0.0 copy-start.2
  68.2 1.9 %copy.21 = bf16[256,1024]{1,0:T(8,128)(2,1)} copy(bf16[256,1024]{1,0:T(8,128)(2,1)} %get-tuple-element.12) | data formatting | bytes 1048576
  70.1 0.0 copy-done.2
  70.1 0.0 copy-start.1
  70.1 0.6 copy.22
  70.7 0.2 copy-done.1
  70.9 0.0 copy-start
  70.9 0.6 copy.23
  71.6 0.2 copy-done
  71.8 0.0 copy-start.4
  71.8 0.6 copy.24
  72.4 0.1 copy-done.4
  72.5 0.0 copy-start.3
  72.5 0.6 copy.25
  73.1 0.1 copy-done.3
  73.2 0.6 copy.26
Async XLA Ops:
  68.2 1.9 %copy-start.2 = (bf16[256,128]{1,0:T(8,128)(2,1)S(1)}, bf16[256,128]{1,0:T(8,128)(2,1)}, u32[]{:S(2)}) copy-start(bf16[256,128]{1,0:T(8,128)(2,1)} %get-tuple-element.13) | copy-start | bytes 196612
  70.1 0.9 %copy-start.1 = (bf16[256,128]{1,0:T(8,128)(2,1)S(1)}, bf16[256,128]{1,0:T(8,128)(2,1)}, u32[]{:S(2)}) copy-start(bf16[256,128]{1,0:T(8,128)(2,1)} %get-tuple-element.14) | copy-start | bytes 196612
  70.9 0.9 %copy-start = (bf16[32,1024]{1,0:T(8,128)(2,1)S(1)}, bf16[32,1024]{1,0:T(8,128)(2,1)}, u32[]{:S(2)}) copy-start(bf16[32,1024]{1,0:T(8,128)(2,1)} %get-tuple-element.15) | copy-start | bytes 196612
  71.8 0.7 copy-start.4
  72.5 0.7 copy-start.3

commit v2 on v1

v2 whole, which is shorter than its diff:
```python
from functools import partial

import jax
import jax.numpy as jnp
from jax import lax
from jax.experimental import pallas as pl
from jax.experimental.pallas import tpu as pltpu
from jax.sharding import PartitionSpec as P

HD = 128
BLOCK = 128
LOG2E = 1.4426950408889634
HIDDEN = -1e30
MESH = pl.DeviceIdType.MESH
F32 = jnp.float32
BF16 = jnp.bfloat16


def dot_nt(a, b):
    return lax.dot_general(a, b, (((1,), (1,)), ((), ())), preferred_element_type=F32)


def dot_nn(a, b):
    return jnp.dot(a, b, preferred_element_type=F32)


def fold_max(x):
    return jnp.max(x.reshape(x.shape[0] // 8, 8, x.shape[1]), axis=0)


def fold_sum(x):
    return jnp.sum(x.reshape(x.shape[0] // 8, 8, x.shape[1]), axis=0)


def turned(x):
    return jnp.transpose(x.astype(F32)).astype(BF16)


def kernel(
    ring,
    mask_ref, qc_i, kc_i, vc_i, doc_i, qh_i, kh_i, vh_i, doh_i,
    dqc_o, dkc_o, dvc_o, dqh_o, dkh_o, dvh_o,
    qc, doc, dqc, in_s, kvc, kvh, qdo, ktc, kth, bias_s, e_c, dp_c, s_c, e_h, dp_h, m_h, st, st_f, st_d,
    acc_h, acc_c, dqp, dq_own, dq_r, dq_x, dq_m, xh_r, xc_r, yh_s, yh_r, yc_s, yc_r, zh_s, zh_r,
    a_s, a_r, q_s, q_r, t_s, t_r, d_s, d_r, z_s, z_r, i_s, i_r,
):
    cells = qc.shape[0]
    rows = qh_i.shape[0]
    heads = qc.shape[1] // HD
    half = heads // 2
    wide = heads * HD
    ext = cells + rows
    lines = ring * rows
    scale = HD ** (-0.5)
    factor = scale * LOG2E
    me = lax.axis_index("seq")
    hx = lax.axis_index("head")
    core = me % 2
    pos_z = (me // 2) % ring
    pos_y = me // (2 * ring)

    def peer(a, d, b):
        y = (pos_y + a) % 2
        z = (pos_z + d + ring) % ring
        c = (core + b) % 2
        return ((y * ring + z) * 2 + c, hx)

    def rcopy(src, dst, send, recv, to):
        return pltpu.make_async_remote_copy(
            src_ref=src, dst_ref=dst, send_sem=send, recv_sem=recv,
            device_id=to, device_id_type=MESH,
        )

    barrier = pltpu.get_barrier_semaphore()
    for d in range(1, ring):
        pl.semaphore_signal(barrier, inc=1, device_id=peer(0, d, 0), device_id_type=MESH)
    pl.semaphore_signal(barrier, inc=1, device_id=peer(1, 0, 0), device_id_type=MESH)
    pl.semaphore_signal(barrier, inc=1, device_id=peer(0, 0, 1), device_id_type=MESH)

    side = half * HD
    moves = [
        (kh_i, kvh.at[0, pl.ds(0, rows), pl.ds(0, HD)]),
        (vh_i, kvh.at[0, pl.ds(0, rows), pl.ds(HD, HD)]),
        (kc_i, kvc.at[0, pl.ds(0, cells), pl.ds(0, HD)]),
        (vc_i, kvc.at[0, pl.ds(0, cells), pl.ds(HD, HD)]),
        (kh_i, kvc.at[0, pl.ds(cells, rows), pl.ds(0, HD)]),
        (vh_i, kvc.at[0, pl.ds(cells, rows), pl.ds(HD, HD)]),
    ]
    for p in range(2):
        part = pl.ds(p * side, side)
        moves.append((qh_i.at[:, part], qdo.at[pl.ds(0, rows), pl.ds(p * wide, side)]))
        moves.append((doh_i.at[:, part], qdo.at[pl.ds(0, rows), pl.ds(p * wide + side, side)]))
    moves += [(qc_i, qc), (doc_i, doc)]
    moves = [pltpu.make_async_copy(x, y, in_s.at[n]) for n, (x, y) in enumerate(moves)]
    for cp in moves:
        cp.start()
    for cp in moves[:-2]:
        cp.wait()

    pl.semaphore_wait(barrier, ring + 1)

    order = []
    for d in range(1, ring // 2 + 1):
        order.append(d)
        if ring - d != d:
            order.append(ring - d)

    far = ring // 2
    cut = rows // 2

    def q_send(slot, step, p):
        to = (slot + step) % ring
        low, size, sem = slot * rows, rows, to
        if to == far:
            size = cut
            if step == -1:
                low, sem = low + cut, 0
        shift = step * rows if slot or step == 1 else (ring - 1) * rows
        lanes = pl.ds(p * wide, wide)
        return rcopy(
            qdo.at[pl.ds(low, size), lanes], qdo.at[pl.ds(low + shift, size), lanes],
            q_s.at[p * ring + sem], q_r.at[p * ring + sem], peer(0, step, 0),
        )

    def q_step(k, p):
        for slot, step in ((k, 1), ((ring - k) % ring, -1)):
            if k:
                q_send((slot - step) % ring, step, p).wait_recv()
            q_send(slot, step, p).start()

    def q_last(p):
        q_send(far - 1, 1, p).wait_recv()
        q_send(far + 1, -1, p).wait_recv()

    a_cp = {}
    for d in order:
        a_cp[d] = rcopy(
            kvh.at[0, pl.ds(0, rows)], kvh.at[0, pl.ds(d * rows, rows)],
            a_s.at[d], a_r.at[d], peer(0, d, 0),
        )
        a_cp[d].start()
    c_y = rcopy(kvc.at[0], kvc.at[2], i_s.at[0], i_r.at[0], peer(1, 0, 0))
    c_y.start()
    c_c = rcopy(kvc.at[0], kvc.at[1], i_s.at[1], i_r.at[1], peer(0, 0, 1))
    c_c.start()
    q_step(0, 0)
    q_step(0, 1)

    lane = lax.broadcasted_iota(jnp.int32, (1, cells), 1)
    for a in range(2):
        for d in range(ring):
            y = (pos_y + a) % 2
            z = (pos_z - d + ring) % ring
            block = (y * ring + z) * 2 * rows // BLOCK
            low = jnp.where(mask_ref[0, block] > 0, 0.0, HIDDEN)
            high = jnp.where(mask_ref[1, block] > 0, 0.0, HIDDEN)
            row = jnp.where(lane < BLOCK, low, high)
            bias_s[a, d * rows : (d + 1) * rows, :] = jnp.broadcast_to(row, (rows, cells))
    acc_h[...] = jnp.zeros_like(acc_h)
    acc_c[...] = jnp.zeros_like(acc_c)

    def column(h):
        return pl.ds(pl.multiple_of(h * HD, HD), HD)

    def cell_local(h, carry):
        q, g = qc[:, column(h)], doc[:, column(h)]
        s = dot_nt(kvc[0, 0:cells, 0:HD], q)
        dp = dot_nt(kvc[0, 0:cells, HD : 2 * HD], g)
        m2 = jnp.max(fold_max(s), axis=0, keepdims=True) * factor
        e = jnp.exp2(s * factor - m2)
        e_c[h, 0:cells, :] = e
        dp_c[h, 0:cells, :] = dp
        s_c[h, 0:1, :] = m2
        s_c[h, 8:9, :] = jnp.sum(fold_sum(e), axis=0, keepdims=True)
        s_c[h, 16:17, :] = jnp.sum(fold_sum(e * dp), axis=0, keepdims=True)
        return carry

    def cell_block(ab, h, carry):
        q, g = qc[:, column(h)], doc[:, column(h)]
        base = cells + ab * lines
        s = dot_nt(kvh[ab, :, 0:HD], q)
        dp = dot_nt(kvh[ab, :, HD : 2 * HD], g)
        s = s * factor + bias_s[ab // 2]
        m2 = jnp.max(fold_max(s), axis=0, keepdims=True)
        e = jnp.exp2(s - m2)
        e_c[h, base : base + lines, :] = e
        dp_c[h, base : base + lines, :] = dp
        s_c[h, ab + 1 : ab + 2, :] = m2
        s_c[h, ab + 9 : ab + 10, :] = jnp.sum(fold_sum(e), axis=0, keepdims=True)
        s_c[h, ab + 17 : ab + 18, :] = jnp.sum(fold_sum(e * dp), axis=0, keepdims=True)
        return carry

    def cell_blocks(ab, hooks):
        def body(h, carry):
            for at, step in hooks:

                @pl.when(h == at)
                def _():
                    q_step(*step)

            return cell_block(ab, h, carry)

        lax.fori_loop(0, heads, body, 0)

    for cp in moves[-2:]:
        cp.wait()
    lax.fori_loop(0, heads, cell_local, 0)
    ktc[0] = turned(kvc[0, :, 0:HD])
    for d in order:
        a_cp[d].wait_recv()
    h_y = rcopy(kvh.at[0], kvh.at[2], i_s.at[3], i_r.at[3], peer(1, 0, 0))
    h_y.start()
    h_c = rcopy(kvh.at[0], kvh.at[1], i_s.at[4], i_r.at[4], peer(0, 0, 1))
    h_c.start()
    c_y.wait_recv()
    c_f = rcopy(kvc.at[2], kvc.at[3], i_s.at[2], i_r.at[2], peer(0, 0, 1))
    c_f.start()
    cell_blocks(0, ())
    h_c.wait_recv()
    cell_blocks(1, ((2, (1, 0)), (7, (1, 1))))
    kth[0] = turned(kvh[0, :, 0:HD])
    kth[1] = turned(kvh[1, :, 0:HD])
    c_c.wait_recv()
    ktc[1] = turned(kvc[1, :, 0:HD])
    ktc[2] = turned(kvc[2, :, 0:HD])
    c_f.wait_recv()
    ktc[3] = turned(kvc[3, :, 0:HD])
    h_y.wait_recv()
    h_f = rcopy(kvh.at[2], kvh.at[3], i_s.at[5], i_r.at[5], peer(0, 0, 1))
    h_f.start()
    kth[2] = turned(kvh[2, :, 0:HD])
    cell_blocks(2, ((4, (2, 0)),))
    h_f.wait_recv()
    cell_blocks(3, ((2, (2, 1)),))
    kth[3] = turned(kvh[3, :, 0:HD])

    def cell_grads(h, carry):
        for at, step in ((2, (3, 0)), (4, (3, 1))):

            @pl.when(h == at)
            def _():
                q_step(*step)

        q, g = qc[:, column(h)], doc[:, column(h)]
        tops = s_c[h, 0:5, :]
        best = jnp.max(tops, axis=0, keepdims=True)
        lift = jnp.exp2(tops - best)
        total = jnp.sum(s_c[h, 8:13, :] * lift, axis=0, keepdims=True)
        inner = jnp.sum(s_c[h, 16:21, :] * lift, axis=0, keepdims=True)
        inv = 1.0 / total
        delta = inner * inv
        lift = lift * inv
        w = e_c[h, 0:cells, :] * lift[0:1]
        ds = (w * (dp_c[h, 0:cells, :] - delta)).astype(BF16)
        acc_c[0, 0:cells, 0:HD] += dot_nn(ds, q)
        acc_c[0, 0:cells, HD : 2 * HD] += dot_nn(w.astype(BF16), g)
        dq = dot_nn(ktc[0, :, 0:cells], ds)
        for ab in range(4):
            part = slice(cells + ab * lines, cells + (ab + 1) * lines)
            w = e_c[h, part, :] * lift[ab + 1 : ab + 2]
            ds = (w * (dp_c[h, part, :] - delta)).astype(BF16)
            acc_h[ab, :, 0:HD] += dot_nn(ds, q)
            acc_h[ab, :, HD : 2 * HD] += dot_nn(w.astype(BF16), g)
            dq = dq + dot_nn(kth[ab], ds)
        dqc[:, column(h)] = (jnp.transpose(dq) * scale).astype(BF16)
        return carry

    lax.fori_loop(0, heads, cell_grads, 0)

    dqc_cp = pltpu.make_async_copy(dqc, dqc_o, in_s.at[12])
    dqc_cp.start()
    hx_cp = []
    for a in (1, 0):
        cp = rcopy(acc_h.at[2 * a + 1], xh_r.at[a], i_s.at[6 + a], i_r.at[6 + a], peer(0, 0, 1))
        cp.start()
        hx_cp.append(cp)

    hy_cp = rcopy(yh_s, yh_r, i_s.at[8], i_r.at[8], peer(1, 0, 0))

    def grouped(p, h):
        return (
            qdo[:, pl.ds(pl.multiple_of((p * heads + h) * HD, HD), HD)],
            qdo[:, pl.ds(pl.multiple_of((p * heads + half + h) * HD, HD), HD)],
        )

    def head_stats(p, h, carry):
        q, g = grouped(p, h)
        tops, totals, inners = [], [], []
        for ab in range(4):
            s = dot_nt(kvc[ab, :, 0:HD], q)
            dp = dot_nt(kvc[ab, :, HD : 2 * HD], g)
            m2 = jnp.max(fold_max(s), axis=0, keepdims=True) * factor
            e = jnp.exp2(s * factor - m2)
            e_h[p * half + h, ab * ext : (ab + 1) * ext, :] = e
            dp_h[p * half + h, ab * ext : (ab + 1) * ext, :] = dp
            m_h[p * half + h, ab : ab + 1, :] = m2
            tops.append(m2)
            totals.append(jnp.sum(fold_sum(e), axis=0, keepdims=True))
            inners.append(jnp.sum(fold_sum(e * dp), axis=0, keepdims=True))
        best = jnp.maximum(jnp.maximum(tops[0], tops[1]), jnp.maximum(tops[2], tops[3]))
        total = jnp.zeros_like(best)
        inner = jnp.zeros_like(best)
        for ab in range(4):
            lift = jnp.exp2(tops[ab] - best)
            total = total + totals[ab] * lift
            inner = inner + inners[ab] * lift
        st[p, 0, pl.ds(h, 1), :] = best + jnp.log(total) * LOG2E
        st[p, 0, pl.ds(half + h, 1), :] = inner / total
        return carry

    t_cp = {}
    for p in range(2):
        q_last(p)

        def body(h, carry):
            if p == 0:

                @pl.when(h == half - 1)
                def _():
                    hx_cp[0].wait_recv()
                    yh_s[...] = (acc_h[2] + xh_r[1]).astype(BF16)
                    hy_cp.start()

            return head_stats(p, h, carry)

        lax.fori_loop(0, half, body, 0)
        for d in order:
            t_cp[p, d] = rcopy(
                st.at[p, 0], st.at[p, d], t_s.at[p * ring + d], t_r.at[p * ring + d],
                peer(0, d, 0),
            )
            t_cp[p, d].start()

    def merge(p):
        for d in order:
            t_cp[p, d].wait_recv()
        seen = [st[p, 0]]
        for d in range(1, ring):
            seen.append(pltpu.roll(st[p, d], d * rows, 1))
        best = seen[0][0:half]
        for d in range(1, ring):
            best = jnp.maximum(best, seen[d][0:half])
        total = jnp.zeros_like(best)
        inner = jnp.zeros_like(best)
        for d in range(ring):
            lift = jnp.exp2(seen[d][0:half] - best)
            total = total + lift
            inner = inner + seen[d][half : 2 * half] * lift
        st_f[p, 0:half] = best + jnp.log(total) * LOG2E
        st_d[p, 0:half] = inner / total

    near = 2
    first = (far, 0, near + 1, ring - near - 1, 1, ring - 1)

    def dq_send(key, p, lanes):
        low, size, slot = 0, rows, key
        if key in (1, ring - 1):
            step = -1 if key == 1 else 1
            target = dq_r.at[0 if key == 1 else 1]
        elif key in (near + 1, ring - near - 1):
            step = -1 if key == near + 1 else 1
            target = dq_x.at[0 if key == near + 1 else 1]
        elif key in (far, 0):
            step = -near if key == far else near
            slot, size, low = far, cut, 0 if key == far else cut
            target = dq_x.at[2]
        else:
            step = -near if key == near else near
            target = dq_r.at[2 if key == near else 3]
        if key in (near, ring - near):
            source = dq_m.at[0 if key == near else 1, pl.ds(0, rows), lanes]
        else:
            source = dqp.at[pl.ds(slot * rows + low, size), lanes]
        return rcopy(
            source, target.at[pl.ds(low, size), lanes],
            d_s.at[p * ring + key], d_r.at[p * ring + key], peer(0, step, 0),
        )

    def lanes_of(p):
        return pl.ds(p * side, side)

    def combine(p):
        lanes = lanes_of(p)
        for key in (far, 0, near + 1, ring - near - 1):
            dq_send(key, p, lanes).wait_recv()
        for n in range(2):
            own = dq_own[1 + n, :, lanes] + dq_x[n, :, lanes].astype(F32)
            part = slice(n * cut, (n + 1) * cut)
            rest = slice((1 - n) * cut, (2 - n) * cut)
            dq_m[n, part, lanes] = (own[part] + dq_x[2, part, lanes].astype(F32)).astype(BF16)
            dq_m[n, rest, lanes] = own[rest].astype(BF16)
        for key in (near, ring - near):
            dq_send(key, p, lanes).start()

    def head_grads(p, h, carry):
        q, g = grouped(p, h)
        at = p * half + h
        lift = jnp.exp2(m_h[at, 0:4, :] - st_f[p, pl.ds(h, 1), :])
        delta = st_d[p, pl.ds(h, 1), :]
        dq = jnp.zeros((HD, lines), F32)
        for ab in range(4):
            part = slice(ab * ext, (ab + 1) * ext)
            w = e_h[at, part, :] * lift[ab : ab + 1]
            ds = (w * (dp_h[at, part, :] - delta)).astype(BF16)
            acc_c[ab, :, 0:HD] += dot_nn(ds, q)
            acc_c[ab, :, HD : 2 * HD] += dot_nn(w.astype(BF16), g)
            dq = dq + dot_nn(ktc[ab], ds)
        flat = jnp.transpose(dq) * scale
        for n, slot in enumerate((0, near, ring - near)):
            dq_own[n, :, column(at)] = flat[slot * rows : (slot + 1) * rows]
        dqp[:, column(at)] = flat.astype(BF16)
        for key in first:
            dq_send(key, p, column(at)).start()
        return carry

    hx_cp[1].wait_recv()
    own_h = acc_h[0] + xh_r[0]
    hy_cp.wait_recv()
    own_h = own_h + yh_r[...].astype(F32)
    acc_h[0, 0:rows] = own_h[0:rows]
    zh_s[...] = own_h.astype(BF16)
    z_cp = {}
    for d in order:
        z_cp[d] = rcopy(
            zh_s.at[pl.ds(d * rows, rows)], zh_r.at[d], z_s.at[d], z_r.at[d], peer(0, -d, 0)
        )
        z_cp[d].start()

    merge(0)
    lax.fori_loop(0, half, partial(head_grads, 0), 0)
    merge(1)
    lax.fori_loop(0, half, partial(head_grads, 1), 0)

    cx_cp = []
    for a in (1, 0):
        cp = rcopy(acc_c.at[2 * a + 1], xc_r.at[a], i_s.at[9 + a], i_r.at[9 + a], peer(0, 0, 1))
        cp.start()
        cx_cp.append(cp)
    combine(0)
    cx_cp[0].wait_recv()
    yc_s[...] = (acc_c[2] + xc_r[1]).astype(BF16)
    cy_cp = rcopy(yc_s, yc_r, i_s.at[11], i_r.at[11], peer(1, 0, 0))
    cy_cp.start()

    combine(1)
    cx_cp[1].wait_recv()
    acc_c[0] = acc_c[0] + xc_r[0]

    d_cp = {}
    for p in range(2):
        for key in range(ring):
            d_cp[p, key] = dq_send(key, p, lanes_of(p))
        for key in (1, ring - 1, near, ring - near):
            d_cp[p, key].wait_recv()
    dq = dq_own[0]
    for n in range(4):
        dq = dq + dq_r[n].astype(F32)
    dqh_o[...] = dq.astype(BF16)

    for d in order:
        z_cp[d].wait_recv()
    own_h = acc_h[0, 0:rows]
    for d in range(1, ring):
        own_h = own_h + zh_r[d].astype(F32)
    cy_cp.wait_recv()
    own_c = acc_c[0] + yc_r[...].astype(F32)
    dkc_o[...] = (own_c[0:cells, 0:HD] * scale).astype(BF16)
    dvc_o[...] = own_c[0:cells, HD : 2 * HD].astype(BF16)
    own_h = own_h + own_c[cells:ext]
    dkh_o[...] = (own_h[:, 0:HD] * scale).astype(BF16)
    dvh_o[...] = own_h[:, HD : 2 * HD].astype(BF16)

    dqc_cp.wait()
    for group in (a_cp, z_cp, d_cp, t_cp):
        for cp in group.values():
            cp.wait_send()
    for p in range(2):
        for k in range(far):
            q_send(k, 1, p).wait_send()
            q_send((ring - k) % ring, -1, p).wait_send()
    for cp in [c_y, c_c, c_f, h_y, h_c, h_f, hy_cp, cy_cp] + hx_cp + cx_cp:
        cp.wait_send()


def put_out(*refs):
    count = len(refs) // 2
    sems = refs[-1]
    copies = [
        pltpu.make_async_copy(refs[i], refs[count + i], sems.at[i]) for i in range(count)
    ]
    for cp in copies:
        cp.start()
    for cp in copies:
        cp.wait()


def per_device(ring, q_cells, k_cells, v_cells, do_cells, q_head, k_head, v_head, do_head, vis_mask):
    cells = q_cells.shape[0]
    rows = q_head.shape[0]
    wide = q_cells.shape[1]
    heads = wide // HD
    lines = ring * rows
    half = heads // 2
    ext = cells + rows
    vmem = pl.BlockSpec(memory_space=pltpu.VMEM)
    anywhere = pl.BlockSpec(memory_space=pl.ANY)
    dma = pltpu.SemaphoreType.DMA
    results = pl.pallas_call(
        partial(kernel, ring),
        out_shape=[
            jax.ShapeDtypeStruct((cells, wide), BF16),
            jax.ShapeDtypeStruct((cells, HD), BF16),
            jax.ShapeDtypeStruct((cells, HD), BF16),
            jax.ShapeDtypeStruct((rows, wide), BF16),
            jax.ShapeDtypeStruct((rows, HD), BF16),
            jax.ShapeDtypeStruct((rows, HD), BF16),
        ],
        in_specs=[pl.BlockSpec(memory_space=pltpu.SMEM)] + [anywhere] * 8,
        out_specs=[anywhere] + [vmem] * 5,
        scratch_shapes=[
            pltpu.VMEM((cells, wide), BF16),
            pltpu.VMEM((cells, wide), BF16),
            pltpu.VMEM((cells, wide), BF16),
            dma((13,)),
            pltpu.VMEM((4, ext, 2 * HD), BF16),
            pltpu.VMEM((4, lines, 2 * HD), BF16),
            pltpu.VMEM((lines, 2 * wide), BF16),
            pltpu.VMEM((4, HD, ext), BF16),
            pltpu.VMEM((4, HD, lines), BF16),
            pltpu.VMEM((2, lines, cells), F32),
            pltpu.VMEM((heads, cells + 4 * lines, cells), F32),
            pltpu.VMEM((heads, cells + 4 * lines, cells), F32),
            pltpu.VMEM((heads, 24, cells), F32),
            pltpu.VMEM((heads, 4 * ext, lines), F32),
            pltpu.VMEM((heads, 4 * ext, lines), F32),
            pltpu.VMEM((heads, 8, lines), F32),
            pltpu.VMEM((2, ring, 2 * half, lines), F32),
            pltpu.VMEM((2, 8, lines), F32),
            pltpu.VMEM((2, 8, lines), F32),
            pltpu.VMEM((4, lines, 2 * HD), F32),
            pltpu.VMEM((4, ext, 2 * HD), F32),
            pltpu.VMEM((lines, wide), BF16),
            pltpu.VMEM((3, rows, wide), F32),
            pltpu.VMEM((4, rows, wide), BF16),
            pltpu.VMEM((3, rows, wide), BF16),
            pltpu.VMEM((2, rows, wide), BF16),
            pltpu.VMEM((2, lines, 2 * HD), F32),
            pltpu.VMEM((2, ext, 2 * HD), F32),
            pltpu.VMEM((lines, 2 * HD), BF16),
            pltpu.VMEM((lines, 2 * HD), BF16),
            pltpu.VMEM((ext, 2 * HD), BF16),
            pltpu.VMEM((ext, 2 * HD), BF16),
            pltpu.VMEM((lines, 2 * HD), BF16),
            pltpu.VMEM((ring, rows, 2 * HD), BF16),
        ]
        + [dma((ring,))] * 2
        + [dma((2 * ring,))] * 6
        + [dma((ring,))] * 2
        + [dma((12,))] * 2,
        compiler_params=pltpu.CompilerParams(
            collective_id=0, has_side_effects=True, vmem_limit_bytes=60 * 1024 * 1024
        ),
    )(vis_mask, q_cells, k_cells, v_cells, do_cells, q_head, k_head, v_head, do_head)
    return pl.pallas_call(
        put_out,
        out_shape=[jax.ShapeDtypeStruct(r.shape, r.dtype) for r in results],
        in_specs=[anywhere] * len(results),
        out_specs=[vmem] * len(results),
        scratch_shapes=[dma((len(results),))],
    )(*results)


def solution(mesh):
    both = P("seq", "head")
    return jax.shard_map(
        partial(per_device, mesh.shape["seq"] // 4),
        mesh=mesh,
        in_specs=(both,) * 8 + (P("seq", None),),
        out_specs=(both,) * 6,
        check_vma=False,
    )
```

time: 74.5 us -> 59.5 us (0.80)
  Pallas kernels: 67.5 us -> 58.7 us
  local copies, waits for them, and re-layouts: 5.62 us -> 0 us
    pallas_call x1, Pallas kernels: 67.5 us -> 56.7 us  [per_device(): pl.pallas_call(partial(kernel, ring), out_shape=[jax.ShapeDtypeStruct((ce...]
    unnamed x16 -> x0, local copies, waits for them, and re-layouts: 5.62 us -> none
    pallas_call x0 -> x1, Pallas kernels: none -> 1.95 us  [per_device(): pl.pallas_call(put_out, out_shape=[jax.ShapeDtypeStruct(r.shape, r.dtype)...]
where the time goes in v2:
time: 59.5 us; the launch traced here: 59.3 us
  Pallas kernels  58.7 us (99%)
  between operations  0.64 us (1%)
    pallas_call x1, Pallas kernels, per_device(): pl.pallas_call(partial(kernel, ring), out_shape=[jax.ShapeDtypeStruct((ce...  56.7 us
    pallas_call x1, Pallas kernels, per_device(): pl.pallas_call(put_out, out_shape=[jax.ShapeDtypeStruct(r.shape, r.dtype)...  1.95 us

profile of v2, /device:TPU:1, one launch (start us, length us, event | category | flops | bytes accessed | tf_op | source)
XLA Modules:
  0.0 59.3 jit_solution(13699159094881661870)
XLA Ops:
  0.6 56.7 %shard_map.136 = (bf16[256,1024]{1,0:T(8,128)(2,1)}, bf16[256,128]{1,0:T(8,128)(2,1)}, bf16[256,128]{1,0:T(8,128)(2,1)}, bf16[32,1024]{1,0:T(8,128)(2,1)}, bf16[...) custom-call(s32[2,8]{1,0:T(2,128)} %mask_ref.1, bf16[256,1024]{1,0:T(8,128)(2,1)} %qc_i.1, bf16[256,128]{1,0:T(8,128)(2,1)} %kc_i.1, ...), custom_call_target="tpu_custom_call" | custom-call | tf_op jit(solution)/shard_map/pallas_call | solution.py:508
  57.4 2.0 %shard_map.137 = (bf16[256,1024]{1,0:T(8,128)(2,1)}, bf16[256,128]{1,0:T(8,128)(2,1)}, bf16[256,128]{1,0:T(8,128)(2,1)}, bf16[32,1024]{1,0:T(8,128)(2,1)}, bf16[...) custom-call(bf16[256,1024]{1,0:T(8,128)(2,1)} %get-tuple-element.12.refs_0_, bf16[256,128]{1,0:T(8,128)(2,1)} %get-tuple-element.13.refs_1_, ...), custom_call_target="tpu_custom_call" | custom-call | tf_op jit(solution)/shard_map/pallas_call | solution.py:564

commit v3 on v2

--- a/solution.py
+++ b/solution.py
@@ -40,7 +40,7 @@
     ring,
     mask_ref, qc_i, kc_i, vc_i, doc_i, qh_i, kh_i, vh_i, doh_i,
     dqc_o, dkc_o, dvc_o, dqh_o, dkh_o, dvh_o,
-    qc, doc, dqc, in_s, kvc, kvh, qdo, ktc, kth, bias_s, e_c, dp_c, s_c, e_h, dp_h, m_h, st, st_f, st_d,
+    qc, doc, dqc, in_s, kvc, kvh, qdo, ktc, kth, bias_s, e_0, e_1, dp_0, dp_1, s_c, e_h, dp_h, m_h, st, st_f, st_d,
     acc_h, acc_c, dqp, dq_own, dq_r, dq_x, dq_m, xh_r, xc_r, yh_s, yh_r, yc_s, yc_r, zh_s, zh_r,
     a_s, a_r, q_s, q_r, t_s, t_r, d_s, d_r, z_s, z_r, i_s, i_r,
 ):
@@ -162,49 +162,55 @@
     def column(h):
         return pl.ds(pl.multiple_of(h * HD, HD), HD)
 
-    def cell_local(h, carry):
-        q, g = qc[:, column(h)], doc[:, column(h)]
-        s = dot_nt(kvc[0, 0:cells, 0:HD], q)
-        dp = dot_nt(kvc[0, 0:cells, HD : 2 * HD], g)
-        m2 = jnp.max(fold_max(s), axis=0, keepdims=True) * factor
-        e = jnp.exp2(s * factor - m2)
-        e_c[h, 0:cells, :] = e
-        dp_c[h, 0:cells, :] = dp
-        s_c[h, 0:1, :] = m2
-        s_c[h, 8:9, :] = jnp.sum(fold_sum(e), axis=0, keepdims=True)
-        s_c[h, 16:17, :] = jnp.sum(fold_sum(e * dp), axis=0, keepdims=True)
-        return carry
-
-    def cell_block(ab, h, carry):
-        q, g = qc[:, column(h)], doc[:, column(h)]
-        base = cells + ab * lines
-        s = dot_nt(kvh[ab, :, 0:HD], q)
-        dp = dot_nt(kvh[ab, :, HD : 2 * HD], g)
-        s = s * factor + bias_s[ab // 2]
-        m2 = jnp.max(fold_max(s), axis=0, keepdims=True)
-        e = jnp.exp2(s - m2)
-        e_c[h, base : base + lines, :] = e
-        dp_c[h, base : base + lines, :] = dp
-        s_c[h, ab + 1 : ab + 2, :] = m2
-        s_c[h, ab + 9 : ab + 10, :] = jnp.sum(fold_sum(e), axis=0, keepdims=True)
-        s_c[h, ab + 17 : ab + 18, :] = jnp.sum(fold_sum(e * dp), axis=0, keepdims=True)
-        return carry
-
-    def cell_blocks(ab, hooks):
-        def body(h, carry):
+    e_c, dp_c = (e_0, e_1), (dp_0, dp_1)
+
+    def cell_blocks(n, hooks):
+        base = cells + (n - 1) * lines if n else 0
+        size = lines if n else cells
+        part = slice(base, base + size)
+
+        def raw(odd, j):
+            h = 2 * j + odd
+            keys = kvh[n - 1, :, 0:HD] if n else kvc[0, 0:cells, 0:HD]
+            values = kvh[n - 1, :, HD : 2 * HD] if n else kvc[0, 0:cells, HD : 2 * HD]
+            e_c[odd][j, part, :] = dot_nt(keys, qc[:, column(h)])
+            dp_c[odd][j, part, :] = dot_nt(values, doc[:, column(h)])
+
+        def settle(odd, j):
+            h = 2 * j + odd
+            s = e_c[odd][j, part, :] * factor
+            if n:
+                s = s + bias_s[(n - 1) // 2]
+            m2 = jnp.max(fold_max(s), axis=0, keepdims=True)
+            e = jnp.exp2(s - m2)
+            e_c[odd][j, part, :] = e
+            s_c[h, n : n + 1, :] = m2
+            s_c[h, n + 8 : n + 9, :] = jnp.sum(fold_sum(e), axis=0, keepdims=True)
+            inner = jnp.sum(fold_sum(e * dp_c[odd][j, part, :]), axis=0, keepdims=True)
+            s_c[h, n + 16 : n + 17, :] = inner
+
+        def body(j, carry):
             for at, step in hooks:
 
-                @pl.when(h == at)
+                @pl.when(j == at)
                 def _():
                     q_step(*step)
 
-            return cell_block(ab, h, carry)
-
-        lax.fori_loop(0, heads, body, 0)
+            raw(1, j)
+            settle(0, j)
+            raw(0, j + 1)
+            settle(1, j)
+            return carry
+
+        raw(0, 0)
+        lax.fori_loop(0, half - 1, body, 0)
+        raw(1, half - 1)
+        settle(0, half - 1)
+        settle(1, half - 1)
 
     for cp in moves[-2:]:
         cp.wait()
-    lax.fori_loop(0, heads, cell_local, 0)
+    cell_blocks(0, ())
     ktc[0] = turned(kvc[0, :, 0:HD])
     for d in order:
         a_cp[d].wait_recv()
@@ -215,9 +221,10 @@
     c_y.wait_recv()
     c_f = rcopy(kvc.at[2], kvc.at[3], i_s.at[2], i_r.at[2], peer(0, 0, 1))
     c_f.start()
-    cell_blocks(0, ())
+    cell_blocks(1, ())
     h_c.wait_recv()
-    cell_blocks(1, ((2, (1, 0)), (7, (1, 1))))
+    cell_blocks(2, ((1, (1, 0)),))
+    q_step(1, 1)
     kth[0] = turned(kvh[0, :, 0:HD])
     kth[1] = turned(kvh[1, :, 0:HD])
     c_c.wait_recv()
@@ -229,43 +236,52 @@
     h_f = rcopy(kvh.at[2], kvh.at[3], i_s.at[5], i_r.at[5], peer(0, 0, 1))
     h_f.start()
     kth[2] = turned(kvh[2, :, 0:HD])
-    cell_blocks(2, ((4, (2, 0)),))
+    cell_blocks(3, ((2, (2, 0)),))
     h_f.wait_recv()
-    cell_blocks(3, ((2, (2, 1)),))
+    cell_blocks(4, ((1, (2, 1)),))
     kth[3] = turned(kvh[3, :, 0:HD])
 
     def cell_grads(h, carry):
-        for at, step in ((2, (3, 0)), (4, (3, 1))):
+        for at, step in ((1, (3, 0)), (2, (3, 1))):
 
             @pl.when(h == at)
             def _():
                 q_step(*step)
 
-        q, g = qc[:, column(h)], doc[:, column(h)]
-        tops = s_c[h, 0:5, :]
-        best = jnp.max(tops, axis=0, keepdims=True)
-        lift = jnp.exp2(tops - best)
-        total = jnp.sum(s_c[h, 8:13, :] * lift, axis=0, keepdims=True)
-        inner = jnp.sum(s_c[h, 16:21, :] * lift, axis=0, keepdims=True)
-        inv = 1.0 / total
-        delta = inner * inv
-        lift = lift * inv
-        w = e_c[h, 0:cells, :] * lift[0:1]
-        ds = (w * (dp_c[h, 0:cells, :] - delta)).astype(BF16)
-        acc_c[0, 0:cells, 0:HD] += dot_nn(ds, q)
-        acc_c[0, 0:cells, HD : 2 * HD] += dot_nn(w.astype(BF16), g)
-        dq = dot_nn(ktc[0, :, 0:cells], ds)
-        for ab in range(4):
-            part = slice(cells + ab * lines, cells + (ab + 1) * lines)
-            w = e_c[h, part, :] * lift[ab + 1 : ab + 2]
-            ds = (w * (dp_c[h, part, :] - delta)).astype(BF16)
-            acc_h[ab, :, 0:HD] += dot_nn(ds, q)
-            acc_h[ab, :, HD : 2 * HD] += dot_nn(w.astype(BF16), g)
-            dq = dq + dot_nn(kth[ab], ds)
-        dqc[:, column(h)] = (jnp.transpose(dq) * scale).astype(BF16)
+        q = [qc[:, column(2 * h + odd)] for odd in range(2)]
+        g = [doc[:, column(2 * h + odd)] for odd in range(2)]
+        lift, delta, dq = [], [], [None, None]
+        for odd in range(2):
+            tops = s_c[2 * h + odd, 0:5, :]
+            best = jnp.max(tops, axis=0, keepdims=True)
+            up = jnp.exp2(tops - best)
+            total = jnp.sum(s_c[2 * h + odd, 8:13, :] * up, axis=0, keepdims=True)
+            inner = jnp.sum(s_c[2 * h + odd, 16:21, :] * up, axis=0, keepdims=True)
+            inv = 1.0 / total
+            delta.append(inner * inv)
+            lift.append(up * inv)
+        for n in range(5):
+            part = slice(cells + (n - 1) * lines, cells + n * lines) if n else slice(0, cells)
+            turn = kth[n - 1] if n else ktc[0, :, 0:cells]
+            dk, dv = 0.0, 0.0
+            for odd in range(2):
+                w = e_c[odd][h, part, :] * lift[odd][n : n + 1]
+                ds = (w * (dp_c[odd][h, part, :] - delta[odd])).astype(BF16)
+                dk = dk + dot_nn(ds, q[odd])
+                dv = dv + dot_nn(w.astype(BF16), g[odd])
+                more = dot_nn(turn, ds)
+                dq[odd] = more if n == 0 else dq[odd] + more
+            if n:
+                acc_h[n - 1, :, 0:HD] += dk
+                acc_h[n - 1, :, HD : 2 * HD] += dv
+            else:
+                acc_c[0, 0:cells, 0:HD] += dk
+                acc_c[0, 0:cells, HD : 2 * HD] += dv
+        for odd in range(2):
+            dqc[:, column(2 * h + odd)] = (jnp.transpose(dq[odd]) * scale).astype(BF16)
         return carry
 
-    lax.fori_loop(0, heads, cell_grads, 0)
+    lax.fori_loop(0, half, cell_grads, 0)
 
     dqc_cp = pltpu.make_async_copy(dqc, dqc_o, in_s.at[12])
     dqc_cp.start()
@@ -393,24 +409,32 @@
             dq_send(key, p, lanes).start()
 
     def head_grads(p, h, carry):
-        q, g = grouped(p, h)
-        at = p * half + h
-        lift = jnp.exp2(m_h[at, 0:4, :] - st_f[p, pl.ds(h, 1), :])
-        delta = st_d[p, pl.ds(h, 1), :]
-        dq = jnp.zeros((HD, lines), F32)
+        at = p * half + 2 * h
+        both = pl.ds(pl.multiple_of(at * HD, 2 * HD), 2 * HD)
+        qg = [grouped(p, 2 * h + odd) for odd in range(2)]
+        lift, delta, dq = [], [], [None, None]
+        for odd in range(2):
+            lift.append(jnp.exp2(m_h[at + odd, 0:4, :] - st_f[p, pl.ds(2 * h + odd, 1), :]))
+            delta.append(st_d[p, pl.ds(2 * h + odd, 1), :])
         for ab in range(4):
             part = slice(ab * ext, (ab + 1) * ext)
-            w = e_h[at, part, :] * lift[ab : ab + 1]
-            ds = (w * (dp_h[at, part, :] - delta)).astype(BF16)
-            acc_c[ab, :, 0:HD] += dot_nn(ds, q)
-            acc_c[ab, :, HD : 2 * HD] += dot_nn(w.astype(BF16), g)
-            dq = dq + dot_nn(ktc[ab], ds)
-        flat = jnp.transpose(dq) * scale
-        for n, slot in enumerate((0, near, ring - near)):
-            dq_own[n, :, column(at)] = flat[slot * rows : (slot + 1) * rows]
-        dqp[:, column(at)] = flat.astype(BF16)
+            dk, dv = 0.0, 0.0
+            for odd in range(2):
+                w = e_h[at + odd, part, :] * lift[odd][ab : ab + 1]
+                ds = (w * (dp_h[at + odd, part, :] - delta[odd])).astype(BF16)
+                dk = dk + dot_nn(ds, qg[odd][0])
+                dv = dv + dot_nn(w.astype(BF16), qg[odd][1])
+                more = dot_nn(ktc[ab], ds)
+                dq[odd] = more if ab == 0 else dq[odd] + more
+            acc_c[ab, :, 0:HD] += dk
+            acc_c[ab, :, HD : 2 * HD] += dv
+        for odd in range(2):
+            flat = jnp.transpose(dq[odd]) * scale
+            for n, slot in enumerate((0, near, ring - near)):
+                dq_own[n, :, column(at + odd)] = flat[slot * rows : (slot + 1) * rows]
+            dqp[:, column(at + odd)] = flat.astype(BF16)
         for key in first:
-            dq_send(key, p, column(at)).start()
+            dq_send(key, p, both).start()
         return carry
 
     hx_cp[1].wait_recv()
@@ -427,9 +451,9 @@
         z_cp[d].start()
 
     merge(0)
-    lax.fori_loop(0, half, partial(head_grads, 0), 0)
+    lax.fori_loop(0, half // 2, partial(head_grads, 0), 0)
     merge(1)
-    lax.fori_loop(0, half, partial(head_grads, 1), 0)
+    lax.fori_loop(0, half // 2, partial(head_grads, 1), 0)
 
     cx_cp = []
     for a in (1, 0):
@@ -528,8 +552,10 @@
             pltpu.VMEM((4, HD, ext), BF16),
             pltpu.VMEM((4, HD, lines), BF16),
             pltpu.VMEM((2, lines, cells), F32),
-            pltpu.VMEM((heads, cells + 4 * lines, cells), F32),
-            pltpu.VMEM((heads, cells + 4 * lines, cells), F32),
+            pltpu.VMEM((half, cells + 4 * lines, cells), F32),
+            pltpu.VMEM((half, cells + 4 * lines, cells), F32),
+            pltpu.VMEM((half, cells + 4 * lines, cells), F32),
+            pltpu.VMEM((half, cells + 4 * lines, cells), F32),
             pltpu.VMEM((heads, 24, cells), F32),
             pltpu.VMEM((heads, 4 * ext, lines), F32),
             pltpu.VMEM((heads, 4 * ext, lines), F32),

time: 59.5 us -> 57.4 us (0.965)
  Pallas kernels: 58.7 us -> 56.6 us
    pallas_call x1, Pallas kernels: 56.7 us -> 54.6 us  [per_device(): pl.pallas_call(partial(kernel, ring), out_shape=[jax.ShapeDtypeStruct((ce...]
where the time goes in v3:
time: 57.4 us; the launch traced here: 57.2 us
  Pallas kernels  56.6 us (99%)
  between operations  0.64 us (1%)
    pallas_call x1, Pallas kernels, per_device(): pl.pallas_call(partial(kernel, ring), out_shape=[jax.ShapeDtypeStruct((ce...  54.6 us
    pallas_call x1, Pallas kernels, per_device(): pl.pallas_call(put_out, out_shape=[jax.ShapeDtypeStruct(r.shape, r.dtype)...  1.95 us

profile of v3, /device:TPU:1, one launch (start us, length us, event | category | flops | bytes accessed | tf_op | source)
XLA Modules:
  0.0 57.2 jit_solution(11202490390518701071)
XLA Ops:
  0.6 54.6 %shard_map.136 = (bf16[256,1024]{1,0:T(8,128)(2,1)}, bf16[256,128]{1,0:T(8,128)(2,1)}, bf16[256,128]{1,0:T(8,128)(2,1)}, bf16[32,1024]{1,0:T(8,128)(2,1)}, bf16[...) custom-call(s32[2,8]{1,0:T(2,128)} %mask_ref.1, bf16[256,1024]{1,0:T(8,128)(2,1)} %qc_i.1, bf16[256,128]{1,0:T(8,128)(2,1)} %kc_i.1, ...), custom_call_target="tpu_custom_call" | custom-call | tf_op jit(solution)/shard_map/pallas_call | solution.py:532
  55.3 2.0 %shard_map.137 = (bf16[256,1024]{1,0:T(8,128)(2,1)}, bf16[256,128]{1,0:T(8,128)(2,1)}, bf16[256,128]{1,0:T(8,128)(2,1)}, bf16[32,1024]{1,0:T(8,128)(2,1)}, bf16[...) custom-call(bf16[256,1024]{1,0:T(8,128)(2,1)} %get-tuple-element.12.refs_0_, bf16[256,128]{1,0:T(8,128)(2,1)} %get-tuple-element.13.refs_1_, ...), custom_call_target="tpu_custom_call" | custom-call | tf_op jit(solution)/shard_map/pallas_call | solution.py:590

commit v4 on v3

--- a/solution.py
+++ b/solution.py
@@ -408,6 +408,11 @@
         for key in (near, ring - near):
             dq_send(key, p, lanes).start()
 
+    cx_cp = [
+        rcopy(acc_c.at[2 * a + 1], xc_r.at[a], i_s.at[9 + a], i_r.at[9 + a], peer(0, 0, 1))
+        for a in (1, 0)
+    ]
+
     def head_grads(p, h, carry):
         at = p * half + 2 * h
         both = pl.ds(pl.multiple_of(at * HD, 2 * HD), 2 * HD)
@@ -416,7 +421,7 @@
         for odd in range(2):
             lift.append(jnp.exp2(m_h[at + odd, 0:4, :] - st_f[p, pl.ds(2 * h + odd, 1), :]))
             delta.append(st_d[p, pl.ds(2 * h + odd, 1), :])
-        for ab in range(4):
+        for ab in (3, 2, 1, 0):
             part = slice(ab * ext, (ab + 1) * ext)
             dk, dv = 0.0, 0.0
             for odd in range(2):
@@ -425,9 +430,15 @@
                 dk = dk + dot_nn(ds, qg[odd][0])
                 dv = dv + dot_nn(w.astype(BF16), qg[odd][1])
                 more = dot_nn(ktc[ab], ds)
-                dq[odd] = more if ab == 0 else dq[odd] + more
+                dq[odd] = more if ab == 3 else dq[odd] + more
             acc_c[ab, :, 0:HD] += dk
             acc_c[ab, :, HD : 2 * HD] += dv
+            if p == 1 and ab == 3:
+
+                @pl.when(h == half // 2 - 1)
+                def _():
+                    cx_cp[0].start()
+
         for odd in range(2):
             flat = jnp.transpose(dq[odd]) * scale
             for n, slot in enumerate((0, near, ring - near)):
@@ -455,16 +466,12 @@
     merge(1)
     lax.fori_loop(0, half // 2, partial(head_grads, 1), 0)
 
-    cx_cp = []
-    for a in (1, 0):
-        cp = rcopy(acc_c.at[2 * a + 1], xc_r.at[a], i_s.at[9 + a], i_r.at[9 + a], peer(0, 0, 1))
-        cp.start()
-        cx_cp.append(cp)
-    combine(0)
+    cx_cp[1].start()
     cx_cp[0].wait_recv()
     yc_s[...] = (acc_c[2] + xc_r[1]).astype(BF16)
     cy_cp = rcopy(yc_s, yc_r, i_s.at[11], i_r.at[11], peer(1, 0, 0))
     cy_cp.start()
+    combine(0)
 
     combine(1)
     cx_cp[1].wait_recv()

time: 57.4 us -> 56.6 us (0.986)
  Pallas kernels: 56.6 us -> 55.8 us
    pallas_call x1, Pallas kernels: 54.6 us -> 53.9 us  [per_device(): pl.pallas_call(partial(kernel, ring), out_shape=[jax.ShapeDtypeStruct((ce...]
where the time goes in v4:
time: 56.6 us; the launch traced here: 56.4 us
  Pallas kernels  55.8 us (99%)
  between operations  0.64 us (1%)
    pallas_call x1, Pallas kernels, per_device(): pl.pallas_call(partial(kernel, ring), out_shape=[jax.ShapeDtypeStruct((ce...  53.9 us
    pallas_call x1, Pallas kernels, per_device(): pl.pallas_call(put_out, out_shape=[jax.ShapeDtypeStruct(r.shape, r.dtype)...  1.95 us

profile of v4, /device:TPU:1, one launch (start us, length us, event | category | flops | bytes accessed | tf_op | source)
XLA Modules:
  0.0 56.4 jit_solution(16003640015346579777)
XLA Ops:
  0.6 53.9 %shard_map.136 = (bf16[256,1024]{1,0:T(8,128)(2,1)}, bf16[256,128]{1,0:T(8,128)(2,1)}, bf16[256,128]{1,0:T(8,128)(2,1)}, bf16[32,1024]{1,0:T(8,128)(2,1)}, bf16[...) custom-call(s32[2,8]{1,0:T(2,128)} %mask_ref.1, bf16[256,1024]{1,0:T(8,128)(2,1)} %qc_i.1, bf16[256,128]{1,0:T(8,128)(2,1)} %kc_i.1, ...), custom_call_target="tpu_custom_call" | custom-call | tf_op jit(solution)/shard_map/pallas_call | solution.py:539
  54.5 2.0 %shard_map.137 = (bf16[256,1024]{1,0:T(8,128)(2,1)}, bf16[256,128]{1,0:T(8,128)(2,1)}, bf16[256,128]{1,0:T(8,128)(2,1)}, bf16[32,1024]{1,0:T(8,128)(2,1)}, bf16[...) custom-call(bf16[256,1024]{1,0:T(8,128)(2,1)} %get-tuple-element.12.refs_0_, bf16[256,128]{1,0:T(8,128)(2,1)} %get-tuple-element.13.refs_1_, ...), custom_call_target="tpu_custom_call" | custom-call | tf_op jit(solution)/shard_map/pallas_call | solution.py:597
